TPU v7x, 512 devices: a whole 4x8x8 slice. The times are simulated.
512 devices in a mesh: samp: 32 (over x, y_lo, core), var: 16 (over z, y_hi).
Axes of the slice: x: 4, y: 8 (y_hi: 2, y_lo: 4; y = y_hi * 4 + y_lo), z: 8, core: 2. Of those that a mesh axis runs over, the one named last changes fastest.
Arguments:
- genotypes: bfloat16 [16384, 40960], P('samp', 'var'), may hold values from 0 to 2, as said below
- imputed: bfloat16 [16384, 20480], P('samp', 'var'), may hold values from 0 to 2, as said below
- centre: int32 [16384], P('samp'), may hold values from 0 to 21, as said below
- phenotypes: float32 [8, 16384], P(None, 'samp'), may hold values from -6 to 6
- earlier: float32 [8, 16384], P(None, 'samp'), may hold values from -6 to 6
- genetic: float32 [8], replicated, may hold values from 0.2 to 2
- noise: float32 [8], replicated, may hold values from 0.2 to 2
Outputs:
- solution: float32 [8, 16384], P(None, ('samp', 'var'))
- residual: float32 [8, 16384], P(None, ('samp', 'var'))
- scores: float32 [8, 20480], P(None, 'var')
Inputs may be any that keep to these rules, and one draw needn't show every extreme that they name: `genotypes`: allele dosages 0, 1 or 2; every variant has its own allele frequency. `imputed`: allele dosages 0, 1 or 2; every variant has its own allele frequency. One of 22 centres; a centre may have no samples.
All inputs are finite; a program needn't handle non-finite values.
Results may differ from a plain program's by a relative error of at most 0.033.
Values may be sent and summed in bfloat16 or wider, within the bound.
No kernel may reach another device: no remote copies, remote signals or barrier semaphores. Data moves between devices by JAX's collectives and lax.ppermute only.
A program may use at most 64 MiB of HBM per device.

v0:
```python
import jax
import jax.numpy as jnp
from jax import lax
from jax.sharding import PartitionSpec as P

M = 40960
CENTRES = 22
ITERS = 2


def inner(values):
    return lax.psum((values[0],), "samp")


def operate(direction, standard, genetic, noise):
    low = direction.astype(jnp.bfloat16)
    partial_proj = jnp.dot(low, standard, preferred_element_type=jnp.float32)
    scale_row = (genetic / M)[:, None]
    summed_proj = lax.psum(partial_proj, "samp")
    scaled = (summed_proj * scale_row).astype(jnp.bfloat16)
    partial_back = lax.dot_general(
        scaled, standard, (((1,), (1,)), ((), ())), preferred_element_type=jnp.float32
    )
    back = lax.psum(partial_back, "var")
    return back + noise[:, None] * direction


def shards(genotypes, imputed, centre, phenotypes, earlier, genetic, noise):
    rows = genotypes.shape[0]
    total = rows * lax.axis_size("samp")
    share = rows // lax.axis_size("var")
    offset = lax.axis_index("var") * share
    values = genotypes.astype(jnp.float32)
    dosage = imputed.astype(jnp.float32)
    onehot = (centre[:, None] == jnp.arange(CENTRES, dtype=jnp.int32)[None, :]).astype(jnp.float32)
    sums = lax.psum(
        (
            jnp.sum(values, axis=0),
            jnp.sum(values * values, axis=0),
            jnp.sum(dosage, axis=0),
            jnp.sum(dosage * dosage, axis=0),
            jnp.dot(earlier, dosage, precision=lax.Precision.HIGHEST),
            jnp.dot(phenotypes, onehot, precision=lax.Precision.HIGHEST),
            jnp.sum(onehot, axis=0),
            jnp.sum(earlier, axis=1),
            jnp.sum(earlier * earlier, axis=1),
        ),
        "samp",
    )
    gen_sum, gen_sq, imp_sum, imp_sq, imp_cross, centre_sum, counts, earlier_sum, earlier_sq = sums
    mean_col = gen_sum / total
    var_col = gen_sq / total - mean_col * mean_col
    standard = ((values - mean_col[None, :]) * lax.rsqrt(var_col + 1e-05)[None, :]).astype(
        jnp.bfloat16
    )
    imp_mean = imp_sum / total
    imp_var = imp_sq / total - imp_mean * imp_mean + 1e-05
    earlier_var = earlier_sq / total + 1e-05
    cross = imp_cross - earlier_sum[:, None] * imp_mean[None, :]
    scores = cross / jnp.sqrt(total * imp_var[None, :] * earlier_var[:, None])
    centre_mean = centre_sum / jnp.maximum(counts, 1.0)[None, :]
    centred = phenotypes - jnp.dot(centre_mean, onehot.T, precision=lax.Precision.HIGHEST)
    solution = jnp.zeros_like(centred)
    residual = centred
    direction = residual
    (norm_now,) = inner((jnp.sum(residual * residual, axis=1),))
    for step in range(ITERS):
        image = operate(direction, standard, genetic, noise)
        (curve,) = inner((jnp.sum(direction * image, axis=1),))
        alpha = norm_now / curve
        solution = solution + alpha[:, None] * direction
        residual = residual - alpha[:, None] * image
        if step + 1 < ITERS:
            (norm_next,) = inner((jnp.sum(residual * residual, axis=1),))
            direction = residual + (norm_next / norm_now)[:, None] * direction
            norm_now = norm_next
    solution = lax.dynamic_slice_in_dim(solution, offset, share, 1)
    residual = lax.dynamic_slice_in_dim(residual, offset, share, 1)
    return (solution, residual, scores)


def solution(mesh):
    in_specs = (
        P("samp", "var"),
        P("samp", "var"),
        P("samp"),
        P(None, "samp"),
        P(None, "samp"),
        P(),
        P(),
    )
    out_specs = (P(None, ("samp", "var")), P(None, ("samp", "var")), P(None, "var"))
    return jax.shard_map(shards, mesh=mesh, in_specs=in_specs, out_specs=out_specs, check_vma=False)
```

profile of v0, /device:TPU:1, one launch (start us, length us, event | category | flops | bytes accessed | tf_op | source)
XLA Modules:
  0.0 1122.3 jit_solution(7656716114734789581)
XLA Ops:
  7.2 2.5 convert_reduce_fusion
  9.8 0.1 convert_reduce_fusion.2
  9.9 0.1 convolution_bitcast_fusion
  10.1 134.2 %all-reduce.2 = (f32[8,22]{0,1:T(8,128)S(1)}, f32[22]{0:T(128)S(1)}, f32[2560]{0:T(1024)S(1)}, f32[2560]{0:T(1024)S(1)}) all-reduce(f32[8,22]{0,1:T(8,128)S(1)} %convolution_bitcast_fusion, f32[22]{0:T(128)S(1)} %convert_reduce_fusion.2, f32[2560]{0:T(1024)S(1)} %get-tuple-element.4, ...), channel_id=1, replica_groups=mesh['samp'=32,'var'=16] {'samp'}, use_global_device_ids=true, to_apply=%region_0.0 | all-reduce | flops 5318 | bytes 42544 | tf_op jit(solution)/shard_map/psum | solution.py:36
  144.2 0.3 convolution_subtract_fusion
  144.5 3.1 fusion.10
  147.7 0.6 fusion.22
  148.3 0.4 convert_reduce_fusion.1
  148.7 253.0 %all-reduce.6.cloned.1.call-done = f32[8,2560]{1,0:T(8,128)} async-done(((f32[8,2560]{1,0:T(8,128)}), f32[8,2560]{1,0:T(8,128)}) %all-reduce.6.cloned.1.call-update) | async-done | bytes 81936 | tf_op jit(solution)/shard_map/psum | solution.py:19
  401.8 2.6 fusion.8
  404.3 85.0 %psum.125 = f32[8,512]{1,0:T(8,128)S(1)} all-reduce(f32[8,512]{1,0:T(8,128)S(1)} %fusion.8), channel_id=1, replica_groups=mesh['samp'=32,'var'=16] {'var'}, use_global_device_ids=true, to_apply=%region_10.0 | all-reduce | flops 4096 | bytes 32768 | tf_op jit(solution)/shard_map/psum | solution.py:24
  489.3 0.2 multiply_reduce_fusion.3
  489.5 84.1 %all-reduce.1 = (f32[8]{0:T(128)S(1)}, f32[8]{0:T(128)S(1)}) all-reduce(f32[8]{0:T(128)S(1)} %get-tuple-element.10, f32[8]{0:T(128)S(1)} %get-tuple-element.9), channel_id=1, replica_groups=mesh['samp'=32,'var'=16] {'samp'}, use_global_device_ids=true, to_apply=%region_4.0 | all-reduce | flops 16 | bytes 128 | tf_op jit(solution)/shard_map/psum | solution.py:12
  573.6 0.2 multiply_reduce_fusion.2
  573.8 67.4 %psum.127 = f32[8]{0:T(128)S(1)} all-reduce(f32[8]{0:T(128)S(1)} %get-tuple-element.25), channel_id=1, replica_groups=mesh['samp'=32,'var'=16] {'samp'}, use_global_device_ids=true, to_apply=%region_14.0 | all-reduce | flops 8 | bytes 64 | tf_op jit(solution)/shard_map/psum | solution.py:12
  641.3 1.3 fusion.6
  642.6 0.1 fusion.21
  642.8 239.9 %all-reduce.8.cloned.1.call-done = f32[8,2560]{1,0:T(8,128)} async-done(((f32[8,2560]{1,0:T(8,128)}), f32[8,2560]{1,0:T(8,128)}) %all-reduce.8.cloned.1.call-update) | async-done | bytes 81936 | tf_op jit(solution)/shard_map/psum | solution.py:19
  882.7 1.7 fusion.4
  884.3 85.0 %psum.129 = f32[8,512]{1,0:T(8,128)S(1)} all-reduce(f32[8,512]{1,0:T(8,128)S(1)} %fusion.4), channel_id=1, replica_groups=mesh['samp'=32,'var'=16] {'var'}, use_global_device_ids=true, to_apply=%region_16.0 | all-reduce | flops 4096 | bytes 32768 | tf_op jit(solution)/shard_map/psum | solution.py:24
  969.3 0.2 multiply_reduce_fusion.1
  969.5 144.5 %all-reduce = (f32[8]{0:T(128)S(1)}, f32[8,1280]{1,0:T(8,128)S(1)}, f32[8]{0:T(128)S(1)}, f32[1280]{0:T(1024)S(1)}, f32[1280]{0:T(1024)S(1)}, /*index=5*/f32[8]{0:T(128)S(1)}) all-reduce(f32[8]{0:T(128)S(1)} %get-tuple-element.23, f32[8,1280]{1,0:T(8,128)S(1)} %fusion.22, ...), channel_id=1, replica_groups=mesh['samp'=32,'var'=16] {'samp'}, use_global_device_ids=true, to_apply=%region_18.0 | all-reduce | flops 12824 | bytes 102592 | tf_op jit(solution)/shard_map/psum | solution.py:12
  1114.0 0.7 dynamic-slice_subtract_fusion
  1114.7 0.7 rsqrt_multiply_fusion
  (27 shorter events, 0.3 us)
Async XLA Ops:
  7.2 2.6 copy-start.4
  7.2 2.7 copy-start.3
  7.2 394.6 %all-reduce.6.cloned.1.call-start = ((), (), s32[]{:S(2)}) async-start(), calls=%async_computation | async-start | bytes 163840 | tf_op jit(solution)/shard_map/psum | solution.py:19
  9.8 137.9 %copy-start.6 = (f32[8]{0:T(128)S(1)}, f32[8]{0:T(128)}, u32[]{:S(2)}) copy-start(f32[8]{0:T(128)} %param.12) | copy-start | bytes 100
  9.8 137.9 %copy-start = (bf16[512,1280]{1,0:T(8,128)(2,1)S(1)}, bf16[512,1280]{1,0:T(8,128)(2,1)}, u32[]{:S(2)}) copy-start(bf16[512,1280]{1,0:T(8,128)(2,1)} %param.8) | copy-start | bytes 3932164
  9.8 137.9 %copy-start.2 = (f32[8,512]{1,0:T(8,128)S(1)}, f32[8,512]{1,0:T(8,128)}, u32[]{:S(2)}) copy-start(f32[8,512]{1,0:T(8,128)} %param.11) | copy-start | bytes 49156
  147.6 735.1 %all-reduce.8.cloned.1.call-start = ((), (), s32[]{:S(2)}) async-start(), calls=%async_computation.1 | async-start | bytes 163840 | tf_op jit(solution)/shard_map/psum | solution.py:19
  148.3 341.0 %copy-start.5 = (f32[8]{0:T(128)S(1)}, f32[8]{0:T(128)}, u32[]{:S(2)}) copy-start(f32[8]{0:T(128)} %param.13) | copy-start | bytes 100
  148.7 492.6 %copy-start.1 = (bf16[512,2560]{1,0:T(8,128)(2,1)S(1)}, bf16[512,2560]{1,0:T(8,128)(2,1)}, u32[]{:S(2)}) copy-start(bf16[512,2560]{1,0:T(8,128)(2,1)} %param.7) | copy-start | bytes 7864324
Sparse Core Ops, SparseCore 0:
  147.7 253.9 all-reduce.5
  642.8 239.8 all-reduce.7
where the time goes:
time: 1120 us
  blocking collectives  600 us (54%)
  waiting for transfers between devices  493 us (44%)
  between operations  14.2 us (1%)
    psum x2, waiting for transfers between devices, operate(): summed_proj = lax.psum(partial_proj, 'samp')  493 us
    psum x3, blocking collectives, inner(): return lax.psum((values[0],), 'samp')  296 us
    psum x2, blocking collectives, operate(): back = lax.psum(partial_back, 'var')  170 us
    psum x1, blocking collectives, shards(): lax.psum((jnp.sum(values, axis=0), jnp.sum(values * values, axis=0), jnp....  134 us
  transfers between devices with their start and end apart: 2, of which 2 were waited for; matrix products, arithmetic and copies ran while one was open for 0% of the time, Pallas kernels for 0%

commit v1 on v0

v1 whole, which is shorter than its diff:
```python
import jax
import jax.numpy as jnp
from jax import lax
from jax.sharding import PartitionSpec as P

M = 40960
CENTRES = 22
SLOTS = 12
LANE = 128
BASE = 4096.0


def split(x, parts):
    out = []
    for _ in range(parts):
        top = lax.reduce_precision(x, 8, 7)
        out.append(top.astype(jnp.bfloat16))
        x = x - top
    return out


def exact_dot(x, y, parts=3):
    pieces = jnp.concatenate(split(x, parts), axis=0)
    full = jnp.dot(pieces, y, preferred_element_type=jnp.float32)
    return jnp.sum(full.reshape(parts, x.shape[0], -1), axis=0)


def exchange(x, axis):
    return lax.all_to_all(x, axis, 0, 0, tiled=True)


def share(x, axis):
    return exchange(jnp.broadcast_to(x[None], (lax.axis_size(axis),) + x.shape), axis)


def in_lanes(columns):
    rows = columns[0].shape[0]
    lane = lax.broadcasted_iota(jnp.int32, (rows, LANE), 1)
    out = jnp.zeros((rows, LANE), jnp.float32)
    for at, column in enumerate(columns):
        out = jnp.where(lane == at, column, out)
    return out


def blocks(x):
    rows, columns = x.shape
    return x.reshape(rows, columns // LANE, LANE).transpose(1, 0, 2)


def flat(x):
    count, rows, _ = x.shape
    return x.transpose(1, 0, 2).reshape(rows, count * LANE)


def shards(genotypes, imputed, centre, phenotypes, earlier, genetic, noise):
    rows, model = genotypes.shape
    other = imputed.shape[1]
    pheno = phenotypes.shape[0]
    groups = lax.axis_size("samp")
    total = rows * groups
    model_blocks, other_blocks = model // LANE, other // LANE
    spare = groups - model_blocks - other_blocks
    me, mine = lax.axis_index("samp"), lax.axis_index("var")
    genetic = genetic[:, None] / M
    noise = noise[:, None]
    bf16, f32 = jnp.bfloat16, jnp.float32

    hot = centre[None, :] == lax.broadcasted_iota(jnp.int32, (2 * SLOTS, rows), 0)
    pairs = jnp.where(hot[:SLOTS], 1.0, jnp.where(hot[SLOTS:], BASE, 0.0)).astype(bf16)
    pieces = jnp.concatenate(split(phenotypes, 3) + [pairs], axis=0)
    product = jnp.dot(pieces, genotypes, preferred_element_type=f32)
    by_model = product[:pheno] + product[pheno : 2 * pheno] + product[2 * pheno : 3 * pheno]
    packed = product[3 * pheno :]
    square_row = jnp.where(lax.broadcasted_iota(jnp.int32, (SLOTS, rows), 0) == CENTRES - SLOTS, BASE, 0.0)
    packed = packed + jnp.dot(square_row.astype(bf16), genotypes * genotypes, preferred_element_type=f32)
    lane = lax.broadcasted_iota(jnp.int32, (rows, LANE), 1)
    spots = [(lane == centre[:, None] + at).astype(bf16) for at in (0, 32, 64)]
    half = pheno // 2
    table = (
        exact_dot(phenotypes[:half], spots[0])
        + exact_dot(phenotypes[half:], spots[1])
        + jnp.dot(jnp.ones((half, rows), bf16), spots[2], preferred_element_type=f32)
    )
    by_other = exact_dot(earlier, imputed)
    dosage = imputed.astype(f32)
    other_sum = jnp.sum(dosage, axis=0, keepdims=True)
    other_sq = jnp.sum(dosage * dosage, axis=0, keepdims=True)
    moments = in_lanes([jnp.sum(earlier, 1, keepdims=True), jnp.sum(earlier * earlier, 1, keepdims=True)])
    first = jnp.concatenate([blocks(by_model), blocks(packed)], axis=1)
    second = jnp.concatenate(
        [
            blocks(by_other),
            jnp.broadcast_to(moments[None], (other_blocks, pheno, LANE)),
            blocks(jnp.concatenate([other_sum, other_sq, other_sum, other_sq], axis=0)),
        ],
        axis=1,
    )
    chunk = jnp.concatenate([first, second, jnp.zeros((spare,) + first.shape[1:], f32)], axis=0)
    chunk = jnp.concatenate([chunk, jnp.broadcast_to(table[None], (groups, half, LANE))], axis=1)
    got = exchange(chunk, "samp")

    raw = jnp.sum(got, axis=0)
    high = jnp.floor(got[:, pheno : pheno + SLOTS] * (1.0 / BASE))
    low = got[:, pheno : pheno + SLOTS] - BASE * high
    counts = jnp.concatenate([jnp.sum(low, axis=0), jnp.sum(high, axis=0)], axis=0)
    table = raw[-half:]
    centre_sum = jnp.concatenate([table[:, :CENTRES], table[:, 32 : 32 + CENTRES]], axis=0)
    centre_count = table[:1, 64 : 64 + CENTRES]
    centre_mean = centre_sum / jnp.maximum(centre_count, 1.0)
    left = jnp.sum(centre_sum - centre_mean * centre_count, axis=1, keepdims=True)
    per_centre = counts[:CENTRES]
    mean = jnp.sum(per_centre, axis=0, keepdims=True) / total
    scale = lax.rsqrt(counts[CENTRES : CENTRES + 1] / total - mean * mean + 1e-05)
    proj0 = raw[:pheno] - jnp.dot(centre_mean, per_centre, precision=lax.Precision.HIGHEST)
    proj0 = (proj0 - left * mean) * scale
    back0 = lax.reduce_precision(proj0 * scale * genetic, 8, 7)
    shift0 = jnp.sum(back0 * mean, axis=1, keepdims=True)

    cross, moments = raw[:pheno], raw[pheno : 2 * pheno]
    other_mean = raw[2 * pheno : 2 * pheno + 1] / total
    other_var = raw[2 * pheno + 1 : 2 * pheno + 2] / total - other_mean * other_mean + 1e-05
    earlier_var = moments[:, 1:2] / total + 1e-05
    score = (cross - moments[:, :1] * other_mean) / jnp.sqrt(total * other_var * earlier_var)

    owner = me < model_blocks
    top = jnp.where(owner, back0, lax.reduce_precision(score, 8, 7))
    shift_parts = [x.astype(f32) for x in split(shift0, 3)]
    rest = jnp.where(owner, in_lanes(shift_parts), score - lax.reduce_precision(score, 8, 7))
    got = share(jnp.concatenate([top, rest], axis=0).astype(bf16), "samp")
    scores = flat(
        got[model_blocks : model_blocks + other_blocks, :pheno].astype(f32)
        + got[model_blocks : model_blocks + other_blocks, pheno:].astype(f32)
    )

    def back(got):
        values = flat(got[:model_blocks, :pheno])
        extra = jnp.sum(got[:model_blocks, pheno:].astype(f32), axis=0)
        part = lax.dot_general(values, genotypes, (((1,), (1,)), ((), ())), preferred_element_type=f32)
        return part - jnp.sum(extra[:, :3], axis=1, keepdims=True), extra

    part, _ = back(got)
    hot = (centre[None, :] == lax.broadcasted_iota(jnp.int32, (CENTRES, rows), 0)).astype(f32)
    start = phenotypes - jnp.dot(centre_mean, hot, precision=lax.Precision.HIGHEST)
    image = jnp.sum(share(part, "var"), axis=0)

    image_low = lax.reduce_precision(image, 8, 7)
    by_model = blocks(jnp.dot(image_low.astype(bf16), genotypes, preferred_element_type=f32))
    by_model = jnp.concatenate([by_model, jnp.zeros((groups - model_blocks, pheno, LANE), f32)], axis=0)
    grams = in_lanes(
        [jnp.sum(x, axis=1, keepdims=True) for x in (start * start, start * image, image * image, image_low)]
    )
    grams = jnp.broadcast_to(grams[None], (groups, pheno, LANE))
    raw = jnp.sum(exchange(jnp.concatenate([by_model, grams], axis=1), "samp"), axis=0)
    gram = [raw[pheno:, at : at + 1] for at in range(4)]
    norm0 = gram[0]
    rate = gram[1] / norm0
    alpha0 = 1.0 / (rate + noise)
    norm1 = alpha0 * alpha0 * (gram[2] - rate * gram[1])
    on_image, on_start = -alpha0, alpha0 * rate + norm1 / norm0
    length = on_image * on_image * gram[2] + 2.0 * on_image * on_start * gram[1] + on_start * on_start * norm0
    proj1 = (raw[:pheno] - gram[3] * mean) * scale
    proj = on_image * proj1 + on_start * proj0
    back1 = lax.reduce_precision(proj * scale * genetic, 8, 7)
    shift1 = jnp.sum(back1 * mean, axis=1, keepdims=True)
    energy = jnp.sum(proj * proj, axis=1, keepdims=True) * genetic
    rest = in_lanes([x.astype(f32) for x in split(shift1, 3) + split(energy, 3)])
    got = share(jnp.concatenate([back1, rest], axis=0).astype(bf16), "samp")

    part, extra = back(got)
    energy = jnp.sum(extra[:, 3:6], axis=1, keepdims=True)
    ways = lax.axis_size("var")
    width = rows // ways
    per = LANE // width
    tiles = blocks(part)
    lane = lax.broadcasted_iota(jnp.int32, (ways, pheno, LANE), 2)
    peer = lax.broadcasted_iota(jnp.int32, (ways, pheno, LANE), 0)
    tiles = jnp.broadcast_to(tiles[:, None], (ways // per, per, pheno, LANE)).reshape(ways, pheno, LANE)
    spot = lax.rem(width * lax.rem(peer, per) + width, LANE)
    got = jnp.sum(exchange(jnp.where(lane == spot, energy[None], tiles), "var"), axis=0)
    lane = lax.broadcasted_iota(jnp.int32, (pheno, LANE), 1)
    offset = width * lax.rem(mine, per)
    curve = jnp.sum(jnp.where(lane == lax.rem(offset + width, LANE), got, 0.0), axis=1, keepdims=True)
    last = lax.dynamic_slice_in_dim(got, offset, width, 1)
    start = lax.dynamic_slice_in_dim(start, mine * width, width, 1)
    image = lax.dynamic_slice_in_dim(image, mine * width, width, 1)
    alpha1 = norm1 / (curve + noise * length)
    direction = on_image * image + on_start * start
    residual = -alpha0 * (image - rate * start) - alpha1 * (last + noise * direction)
    return (alpha0 * start + alpha1 * direction, residual, scores)


def solution(mesh):
    in_specs = (
        P("samp", "var"),
        P("samp", "var"),
        P("samp"),
        P(None, "samp"),
        P(None, "samp"),
        P(),
        P(),
    )
    out_specs = (P(None, ("samp", "var")), P(None, ("samp", "var")), P(None, "var"))
    return jax.shard_map(shards, mesh=mesh, in_specs=in_specs, out_specs=out_specs, check_vma=False)
```

time: 1120 us -> 130 us (0.12)
  blocking collectives: 600 us -> 12.1 us
  waiting for transfers between devices: 493 us -> 57.5 us
  starting transfers between devices: 0.08 us -> 35.9 us
  between operations: 14.2 us -> 0.98 us
    psum x6 -> x0, blocking collectives: 600 us -> none  [the longest x3 296 us: inner(): return lax.psum((values[0],), 'samp')]
    psum x2 -> x0, waiting for transfers between devices: 493 us -> none  [operate(): summed_proj = lax.psum(partial_proj, 'samp')]
    all_to_all x0 -> x5, waiting for transfers between devices: none -> 57.5 us  [exchange(): return lax.all_to_all(x, axis, 0, 0, tiled=True)]
    all_to_all x0 -> x5, starting transfers between devices: none -> 35.9 us  [exchange(): return lax.all_to_all(x, axis, 0, 0, tiled=True)]
    all_to_all x0 -> x1, blocking collectives: none -> 12.1 us  [exchange(): return lax.all_to_all(x, axis, 0, 0, tiled=True)]
  transfers between devices with their start and end apart: 2 -> 5, of which waited for: 2 -> 5; matrix products, arithmetic and copies ran while one was open for 0% -> 1% of each run, Pallas kernels for 0% -> 0%
where the time goes in v1:
time: 130 us; the launch traced here: 129 us
  waiting for transfers between devices  57.5 us (44%)
  starting transfers between devices  35.9 us (28%)
  blocking collectives  12.1 us (9%)
  other arithmetic  11.7 us (9%)
  matrix products  8.38 us (6%)
  local copies, waits for them, and re-layouts  1.82 us (1%)
    all_to_all x5, waiting for transfers between devices, exchange(): return lax.all_to_all(x, axis, 0, 0, tiled=True)  57.5 us
    all_to_all x5, starting transfers between devices, exchange(): return lax.all_to_all(x, axis, 0, 0, tiled=True)  35.9 us
    all_to_all x1, blocking collectives, exchange(): return lax.all_to_all(x, axis, 0, 0, tiled=True)  12.1 us
    dot_general x3, matrix products, exact_dot(): full = jnp.dot(pieces, y, preferred_element_type=jnp.float32)  2.8 us
  transfers between devices with their start and end apart: 5, of which 5 were waited for; matrix products, arithmetic and copies ran while one was open for 1% of the time, Pallas kernels for 0%

profile of v1, /device:TPU:1, one launch (start us, length us, event | category | flops | bytes accessed | tf_op | source)
XLA Modules:
  0.0 128.5 jit_solution(1218678071239887655)
XLA Ops:
  1.3 0.8 iota_compare_fusion.8
  2.2 0.8 reduce-precision_convert_fusion.6
  3.0 0.7 reduce-precision_convert_fusion.3
  3.7 1.7 %convert_reduce_fusion = (f32[1280]{0:T(1024)S(1)}, f32[1280]{0:T(1024)S(1)}) fusion(bf16[512,1280]{1,0:T(8,128)(2,1)} %param.8), kind=kLoop, calls=%fused_computation.2 | loop fusion | flops 2618880 | bytes 1320960 | tf_op jit(solution)/shard_map/reduce_sum | solution.py:86
  5.7 0.9 fusion.7
  6.7 0.9 reduce-precision_convert_fusion.1
  7.6 2.3 %fusion.14 = f32[36,2560]{1,0:T(8,128)S(1)} fusion(bf16[512,2560]{1,0:T(8,128)(2,1)} %param.7, bf16[12,512]{1,0:T(8,128)(2,1)S(1)} %select_convert_fusion, bf16[8,512]{1,0:T(8,128)(2,1)S(1)} %get-tuple-element.31, bf16[8,512]{1,0:T(8,128)(2,1)S(1)} %get-tuple-element.32, bf16[8,512]{1,0:T(8,128)(2,1)S(1)} %get-tuple-element.30), kind=kOutput, calls=%fused_computation.43 | convolution fusion | flops 94519296 | bytes 3026944 | tf_op jit(solution)/shard_map/dot_general | solution.py:71
  10.8 1.6 %fusion.2 = f32[8,1280]{1,0:T(8,128)S(1)} fusion(bf16[512,1280]{1,0:T(8,128)(2,1)} %param.8, bf16[8,512]{1,0:T(8,128)(2,1)S(1)} %get-tuple-element.35, bf16[8,512]{1,0:T(8,128)(2,1)S(1)} %get-tuple-element.34, bf16[8,512]{1,0:T(8,128)(2,1)S(1)} %get-tuple-element.33), kind=kOutput, calls=%fused_computation.6 | convolution fusion | flops 31551488 | bytes 1376256 | tf_op jit(solution)/shard_map/dot_general | solution.py:24
  12.5 0.9 pad_maximum_fusion
  13.4 10.4 %all-to-all-start = ((f32[32,24,128]{2,1,0:T(8,128)}), f32[32,24,128]{2,1,0:T(8,128)S(1)}, u32[]{:S(2)}, u32[]{:S(2)}) async-start(f32[32,24,128]{2,1,0:T(8,128)} %pad_maximum_fusion), calls=%async_computation | async-start | bytes 786432 | tf_op jit(solution)/shard_map/all_to_all | solution.py:29
  23.9 14.1 %all-to-all-done = f32[32,24,128]{2,1,0:T(8,128)S(1)} async-done(((f32[32,24,128]{2,1,0:T(8,128)}), f32[32,24,128]{2,1,0:T(8,128)S(1)}, u32[]{:S(2)}, u32[]{:S(2)}) %all-to-all-start) | async-done | bytes 393248 | tf_op jit(solution)/shard_map/all_to_all | solution.py:29
  39.0 12.1 %all_to_all.30 = bf16[32,16,128]{2,1,0:T(8,128)(2,1)S(1)} all-to-all(bf16[32,16,128]{2,1,0:T(8,128)(2,1)S(1)} %broadcast_in_dim.196), channel_id=1, replica_groups=mesh['samp'=32,'var'=16] {'samp'}, dimensions={0} | all-to-all | bytes 262144 | tf_op jit(solution)/shard_map/all_to_all | solution.py:29
  51.3 0.8 convolution_subtract_fusion.2
  52.1 0.7 broadcast_in_dim.197
  52.8 11.2 %all-to-all-start.2 = ((f32[16,8,512]{2,1,0:T(8,128)}), f32[16,8,512]{2,1,0:T(8,128)S(1)}, u32[]{:S(2)}, u32[]{:S(2)}) async-start(f32[16,8,512]{2,1,0:T(8,128)} %broadcast_in_dim.197), calls=%async_computation.2 | async-start | bytes 524288 | tf_op jit(solution)/shard_map/all_to_all | solution.py:29
  64.0 12.7 %all-to-all-done.2 = f32[16,8,512]{2,1,0:T(8,128)S(1)} async-done(((f32[16,8,512]{2,1,0:T(8,128)}), f32[16,8,512]{2,1,0:T(8,128)S(1)}, u32[]{:S(2)}, u32[]{:S(2)}) %all-to-all-start.2) | async-done | bytes 262176 | tf_op jit(solution)/shard_map/all_to_all | solution.py:29
  78.4 7.2 %all-to-all-start.3 = ((f32[32,16,128]{2,1,0:T(8,128)}), f32[32,16,128]{2,1,0:T(8,128)S(1)}, u32[]{:S(2)}, u32[]{:S(2)}) async-start(f32[32,16,128]{2,1,0:T(8,128)} %select_maximum_fusion), calls=%async_computation.3 | async-start | bytes 524288 | tf_op jit(solution)/shard_map/all_to_all | solution.py:29
  85.7 11.2 %all-to-all-done.3 = f32[32,16,128]{2,1,0:T(8,128)S(1)} async-done(((f32[32,16,128]{2,1,0:T(8,128)}), f32[32,16,128]{2,1,0:T(8,128)S(1)}, u32[]{:S(2)}, u32[]{:S(2)}) %all-to-all-start.3) | async-done | bytes 262176 | tf_op jit(solution)/shard_map/all_to_all | solution.py:29
  98.3 3.6 %all-to-all-start.4 = ((bf16[32,16,128]{2,1,0:T(8,128)(2,1)}), bf16[32,16,128]{2,1,0:T(8,128)(2,1)S(1)}, u32[]{:S(2)}, u32[]{:S(2)}) async-start(bf16[32,16,128]{2,1,0:T(8,128)(2,1)} %broadcast_in_dim.210), calls=%async_computation.4 | async-start | bytes 262144 | tf_op jit(solution)/shard_map/all_to_all | solution.py:29
  102.0 8.7 %all-to-all-done.4 = bf16[32,16,128]{2,1,0:T(8,128)(2,1)S(1)} async-done(((bf16[32,16,128]{2,1,0:T(8,128)(2,1)}), bf16[32,16,128]{2,1,0:T(8,128)(2,1)S(1)}, u32[]{:S(2)}, u32[]{:S(2)}) %all-to-all-start.4) | async-done | bytes 131104 | tf_op jit(solution)/shard_map/all_to_all | solution.py:29
  110.9 0.8 fusion.3
  111.7 0.8 bitcast_select_fusion
  112.4 3.5 %all-to-all-start.5 = ((f32[16,8,128]{2,1,0:T(8,128)}), f32[16,8,128]{2,1,0:T(8,128)S(1)}, u32[]{:S(2)}, u32[]{:S(2)}) async-start(f32[16,8,128]{2,1,0:T(8,128)} %bitcast_select_fusion), calls=%async_computation.5 | async-start | bytes 131072 | tf_op jit(solution)/shard_map/all_to_all | solution.py:29
  116.6 10.9 %all-to-all-done.5 = f32[16,8,128]{2,1,0:T(8,128)S(1)} async-done(((f32[16,8,128]{2,1,0:T(8,128)}), f32[16,8,128]{2,1,0:T(8,128)S(1)}, u32[]{:S(2)}, u32[]{:S(2)}) %all-to-all-start.5) | async-done | bytes 65568 | tf_op jit(solution)/shard_map/all_to_all | solution.py:29
  (81 shorter events, 8.2 us)
Async XLA Ops:
  1.3 8.6 %copy-start = (bf16[512,2560]{1,0:T(8,128)(2,1)S(1)}, bf16[512,2560]{1,0:T(8,128)(2,1)}, u32[]{:S(2)}) copy-start(bf16[512,2560]{1,0:T(8,128)(2,1)} %param.7) | copy-start | bytes 7864324
  10.4 13.4 %copy-start.4 = (f32[8]{0:T(128)S(1)}, f32[8]{0:T(128)}, u32[]{:S(2)}) copy-start(f32[8]{0:T(128)} %param.12) | copy-start | bytes 100
  13.4 24.6 %all-to-all-start = ((f32[32,24,128]{2,1,0:T(8,128)}), f32[32,24,128]{2,1,0:T(8,128)S(1)}, u32[]{:S(2)}, u32[]{:S(2)}) async-start(f32[32,24,128]{2,1,0:T(8,128)} %pad_maximum_fusion), calls=%async_computation | async-start | bytes 786432 | tf_op jit(solution)/shard_map/all_to_all | solution.py:29
  23.8 52.9 %copy-start.1 = (f32[8,512]{1,0:T(8,128)S(1)}, f32[8,512]{1,0:T(8,128)}, u32[]{:S(2)}) copy-start(f32[8,512]{1,0:T(8,128)} %param.10) | copy-start | bytes 49156
  23.9 52.9 %copy-start.2 = (s32[512]{0:T(512)S(1)}, s32[512]{0:T(512)}, u32[]{:S(2)}) copy-start(s32[512]{0:T(512)} %param.9) | copy-start | bytes 6148
  52.1 33.5 %copy-start.3 = (f32[8]{0:T(128)S(1)}, f32[8]{0:T(128)}, u32[]{:S(2)}) copy-start(f32[8]{0:T(128)} %param.13) | copy-start | bytes 100
  52.8 23.9 %all-to-all-start.2 = ((f32[16,8,512]{2,1,0:T(8,128)}), f32[16,8,512]{2,1,0:T(8,128)S(1)}, u32[]{:S(2)}, u32[]{:S(2)}) async-start(f32[16,8,512]{2,1,0:T(8,128)} %broadcast_in_dim.197), calls=%async_computation.2 | async-start | bytes 524288 | tf_op jit(solution)/shard_map/all_to_all | solution.py:29
  78.4 18.5 %all-to-all-start.3 = ((f32[32,16,128]{2,1,0:T(8,128)}), f32[32,16,128]{2,1,0:T(8,128)S(1)}, u32[]{:S(2)}, u32[]{:S(2)}) async-start(f32[32,16,128]{2,1,0:T(8,128)} %select_maximum_fusion), calls=%async_computation.3 | async-start | bytes 524288 | tf_op jit(solution)/shard_map/all_to_all | solution.py:29
  98.3 12.4 %all-to-all-start.4 = ((bf16[32,16,128]{2,1,0:T(8,128)(2,1)}), bf16[32,16,128]{2,1,0:T(8,128)(2,1)S(1)}, u32[]{:S(2)}, u32[]{:S(2)}) async-start(bf16[32,16,128]{2,1,0:T(8,128)(2,1)} %broadcast_in_dim.210), calls=%async_computation.4 | async-start | bytes 262144 | tf_op jit(solution)/shard_map/all_to_all | solution.py:29
  112.4 15.0 %all-to-all-start.5 = ((f32[16,8,128]{2,1,0:T(8,128)}), f32[16,8,128]{2,1,0:T(8,128)S(1)}, u32[]{:S(2)}, u32[]{:S(2)}) async-start(f32[16,8,128]{2,1,0:T(8,128)} %bitcast_select_fusion), calls=%async_computation.5 | async-start | bytes 131072 | tf_op jit(solution)/shard_map/all_to_all | solution.py:29

commit v2 on v0

v2 whole, which is shorter than its diff:
```python
import functools

import jax
import jax.numpy as jnp
from jax import lax
from jax.experimental import pallas as pl
from jax.experimental.pallas import tpu as pltpu
from jax.sharding import PartitionSpec as P

M = 40960
CENTRES = 22
SLOTS = 12
LANE = 128
BASE = 4096.0
STEPS = 5
GRANT = 16 << 20
BF16, F32 = jnp.bfloat16, jnp.float32
NT = (((1,), (1,)), ((), ()))


def split(x, parts):
    out = []
    for _ in range(parts):
        top = x.astype(BF16)
        out.append(top)
        x = x - top.astype(F32)
    return out


def dot(x, y):
    return jnp.dot(x, y, preferred_element_type=F32)


def dot_t(x, y):
    return lax.dot_general(x, y, NT, preferred_element_type=F32)


def iota(shape, dim):
    return lax.broadcasted_iota(jnp.int32, shape, dim)


def row_sum(x):
    return jnp.sum(x, axis=1, keepdims=True)


def in_lanes(columns):
    lane = iota((columns[0].shape[0], LANE), 1)
    out = jnp.zeros((columns[0].shape[0], LANE), F32)
    for at, column in enumerate(columns):
        out = jnp.where(lane == at, column, out)
    return out


def cut(x, at):
    return x[:, at * LANE : (at + 1) * LANE]


def gather_kernel(
    gen_hbm, imp_hbm, centre_hbm, phen_hbm, earl_hbm, genetic_hbm, noise_hbm,
    out_ref, gen_ref, cols_ref, imp_ref, centre_ref, phen_ref, earl_ref, scal_ref, sem,
):
    rows, model = gen_ref.shape
    groups, pheno = out_ref.shape[0], phen_ref.shape[0]
    wide, narrow = model // STEPS, imp_ref.shape[1] // STEPS
    own, other = wide // LANE, narrow // LANE
    first_other = own * STEPS
    small = [(centre_hbm, centre_ref), (phen_hbm, phen_ref), (earl_hbm, earl_ref)]
    small += [(genetic_hbm, scal_ref.at[0]), (noise_hbm, scal_ref.at[1])]
    copies = [pltpu.make_async_copy(x, y, sem.at[i]) for i, (x, y) in enumerate(small)]
    for step in range(STEPS):
        cols = pl.ds(step * wide, wide)
        copies.append(pltpu.make_async_copy(gen_hbm.at[:, cols], gen_ref.at[:, cols], sem.at[5 + 2 * step]))
        cols = pl.ds(step * narrow, narrow)
        copies.append(pltpu.make_async_copy(imp_hbm.at[:, cols], imp_ref.at[:, cols], sem.at[6 + 2 * step]))
    for copy in copies:
        copy.start()

    spot = iota((LANE, rows), 0)
    slot = iota((16, rows), 0)
    for copy in copies[:3]:
        copy.wait()
    centre = centre_ref[...]
    pairs = jnp.where(slot < SLOTS, jnp.where(centre == slot, 1.0, jnp.where(centre == slot + SLOTS, BASE, 0.0)), 0.0)
    pieces = [p.astype(F32) for p in split(phen_ref[...], 3)]
    phen = jnp.concatenate(pieces + [jnp.ones((pheno, rows), F32)], axis=0).astype(BF16)
    left = jnp.concatenate(pieces + [pairs], axis=0).astype(BF16)
    left_square = jnp.where(slot == CENTRES - SLOTS, BASE, 0.0).astype(BF16)
    earl = earl_ref[...]
    pieces = [p.astype(F32) for p in split(earl, 3)]
    right = jnp.concatenate(pieces + [jnp.ones((pheno, rows), F32)], axis=0).astype(BF16)
    right_square = jnp.ones((16, rows), BF16)
    sums = []
    for at in (0, 32, 64):
        full = dot_t(phen, jnp.where(spot == centre + at, 1.0, 0.0).astype(BF16))
        sums.append(full[24:32] if at == 64 else full[0:8] + full[8:16] + full[16:24])
    row = iota((pheno, LANE), 0)
    table = jnp.where(row < 4, 0.0, pltpu.roll(sums[0], 4, 0) + sums[1] + sums[2])
    moments = in_lanes([row_sum(earl), row_sum(earl * earl)])
    for at in range(first_other + other * STEPS, groups):
        out_ref[at, 0:8, :] = jnp.zeros((8, LANE), F32)
        out_ref[at, 8:16, :] = jnp.zeros((8, LANE), F32)
        out_ref[at, 16:24, :] = table
    for copy in copies[3:5]:
        copy.wait()
    for at in range(2):
        column = jnp.zeros((pheno, LANE), F32)
        for k in range(pheno):
            column = jnp.where(row == k, scal_ref[at, k], column)
        cols_ref[at] = column * (1.0 / M) if at == 0 else column

    for step in range(STEPS):
        copies[5 + 2 * step].wait()
        gen = gen_ref[:, step * wide : (step + 1) * wide]
        full = dot(left, gen)
        by_model = full[0:8] + full[8:16] + full[16:24]
        packed = full[24:40] + dot(left_square, gen * gen)
        for at in range(own):
            block = step * own + at
            out_ref[block, 0:8, :] = cut(by_model, at)
            out_ref[block, 8:16, :] = cut(packed[0:8], at)
            out_ref[block, 16:24, :] = cut(packed[8:16], at) + table
        copies[6 + 2 * step].wait()
        imp = imp_ref[:, step * narrow : (step + 1) * narrow]
        full = dot(right, imp)
        by_other = full[0:8] + full[8:16] + full[16:24]
        square = dot(right_square, imp * imp)[0:8]
        for at in range(other):
            block = first_other + step * other + at
            counts = jnp.where(row == 0, cut(full[24:32], at), jnp.where(row == 1, cut(square, at), table))
            out_ref[block, 0:8, :] = cut(by_other, at)
            out_ref[block, 8:16, :] = moments
            out_ref[block, 16:24, :] = counts


def gather(groups, *operands):
    genotypes, imputed, _, phenotypes = operands[:4]
    rows, model = genotypes.shape
    other = imputed.shape[1]
    pheno = phenotypes.shape[0]
    return pl.pallas_call(
        gather_kernel,
        out_shape=[
            pltpu.VMEM((groups, 24, LANE), F32),
            pltpu.VMEM((rows, model), BF16),
            pltpu.VMEM((2, pheno, LANE), F32),
        ],
        in_specs=[pl.BlockSpec(memory_space=pltpu.HBM)] * len(operands),
        out_specs=[pl.BlockSpec(memory_space=pltpu.VMEM)] * 3,
        scratch_shapes=[
            pltpu.VMEM((rows, other), BF16),
            pltpu.VMEM((1, rows), jnp.int32),
            pltpu.VMEM((pheno, rows), F32),
            pltpu.VMEM((pheno, rows), F32),
            pltpu.SMEM((2, pheno), F32),
            pltpu.SemaphoreType.DMA((5 + 2 * STEPS,)),
        ],
        compiler_params=pltpu.CompilerParams(vmem_limit_bytes=GRANT),
    )(*[pltpu.with_memory_space_constraint(x, pltpu.HBM) for x in operands])


def call(kernel, outs, *operands):
    return pl.pallas_call(
        kernel,
        out_shape=[
            jax.ShapeDtypeStruct(shape, kind) if last else pltpu.VMEM(shape, kind) for shape, kind, last in outs
        ],
        in_specs=[pl.BlockSpec(memory_space=pltpu.VMEM)] * len(operands),
        out_specs=[pl.BlockSpec(memory_space=pltpu.VMEM)] * len(outs),
        compiler_params=pltpu.CompilerParams(vmem_limit_bytes=GRANT),
    )(*[pltpu.with_memory_space_constraint(x, pltpu.VMEM) for x in operands])


def owner_kernel(total, model_blocks, got_ref, cols_ref, send_ref, keep_ref):
    groups, pheno = got_ref.shape[0], 8
    got = got_ref[...]
    raw = jnp.sum(got, axis=0)
    pack = got[:, 8:24, :]
    high = jnp.floor(pack * (1.0 / BASE))
    low = jnp.sum(pack - BASE * high, axis=0)
    high = jnp.sum(high, axis=0)
    table = raw[16:24]
    row = iota((pheno, LANE), 0)
    lane = iota((pheno, LANE), 1)
    sums = jnp.where(row < 4, pltpu.roll(table, 4, 0), pltpu.roll(table, LANE - 32, 1))
    sums = jnp.where(lane < CENTRES, sums, 0.0)
    count = pltpu.roll(table, LANE - 64, 1)
    count = jnp.where(row < 4, pltpu.roll(count, 4, 0), count)
    count = jnp.where(lane < CENTRES, count, 0.0)
    centre_mean = sums / jnp.maximum(count, 1.0)
    left = row_sum(sums - centre_mean * count)
    proj = raw[0:8]
    seen = jnp.zeros((1, LANE), F32)
    for c in range(CENTRES):
        line = low[c : c + 1] if c < SLOTS else high[c - SLOTS : c - SLOTS + 1]
        seen = seen + line
        proj = proj - centre_mean[:, c : c + 1] * line
    mean = seen / total
    scale = lax.rsqrt(high[CENTRES - SLOTS : CENTRES - SLOTS + 1] / total - mean * mean + 1e-05)
    proj = (proj - left * mean) * scale
    back = proj * scale * cols_ref[0]
    m0, m1, m2 = [x.astype(F32) for x in split(mean, 3)]
    lines = jnp.where(row == 0, m0, jnp.where(row == 1, m1, jnp.where(row == 2, m2, 0.0)))

    other_mean = raw[16:17] / total
    other_var = raw[17:18] / total - other_mean * other_mean + 1e-05
    moments = raw[8:16]
    earlier_var = moments[:, 1:2] / total + 1e-05
    score = (raw[0:8] - moments[:, 0:1] * other_mean) / jnp.sqrt(total * other_var * earlier_var)
    score_top = score.astype(BF16).astype(F32)

    owner = lax.axis_index("samp") < model_blocks
    send = jnp.concatenate([jnp.where(owner, back, score_top), jnp.where(owner, lines, score - score_top)], axis=0)
    send_ref[...] = jnp.broadcast_to(send.astype(BF16)[None], (groups, 16, LANE))
    keep_ref[0] = proj
    keep_ref[1] = jnp.broadcast_to(mean, (pheno, LANE))
    keep_ref[2] = jnp.broadcast_to(scale, (pheno, LANE))
    keep_ref[3] = centre_mean


def back_product(got_ref, gen_ref, model_blocks):
    acc = None
    for at in range(0, model_blocks, 2):
        values = jnp.concatenate([got_ref[at], got_ref[at + 1]], axis=1)
        part = dot_t(values, gen_ref[:, at * LANE : (at + 2) * LANE])
        acc = part if acc is None else acc + part
    return acc[0:8]


def back0_kernel(model_blocks, other_blocks, got_ref, gen_ref, centre_ref, phen_ref, keep_ref, send_ref, start_ref, mean_ref, score_ref):
    ways = send_ref.shape[0]
    pheno, rows = phen_ref.shape
    shift = jnp.zeros((pheno, LANE), F32)
    for at in range(model_blocks):
        block = got_ref[at].astype(F32)
        mean = block[8:9] + block[9:10] + block[10:11]
        mean_ref[:, at * LANE : (at + 1) * LANE] = mean
        shift = shift + block[0:8] * mean
    part = back_product(got_ref, gen_ref, model_blocks) - row_sum(shift)
    half = rows // 2
    send = jnp.concatenate([part[:, :half], part[:, half:]], axis=0).astype(BF16)
    send_ref[...] = jnp.broadcast_to(send[None], (ways, 16, half))
    for at in range(other_blocks):
        block = got_ref[model_blocks + at].astype(F32)
        score_ref[:, at * LANE : (at + 1) * LANE] = block[0:8] + block[8:16]
    centre = centre_ref[...]
    start = phen_ref[...]
    centre_mean = keep_ref[3]
    for c in range(CENTRES):
        start = start - jnp.where(centre == c, centre_mean[:, c : c + 1], 0.0)
    start_ref[...] = start


def project_kernel(model_blocks, got_ref, gen_ref, start_ref, mean_ref, send_ref, image_ref):
    groups = send_ref.shape[0]
    pheno, rows = start_ref.shape
    half = rows // 2
    both = jnp.sum(got_ref[...].astype(F32), axis=0)
    image = jnp.concatenate([both[0:8], both[8:16]], axis=1)
    image_ref[...] = image
    start = start_ref[...]
    parts = []
    for x in (start * start, start * image, image * image):
        parts += [p.astype(F32) for p in split(row_sum(x), 3)]
    grams = in_lanes(parts)
    total = row_sum(image)
    left = jnp.concatenate([p.astype(F32) for p in split(image, 2)], axis=0).astype(BF16)
    for at in range(0, model_blocks, 4):
        cols = slice(at * LANE, (at + 4) * LANE)
        full = dot(left, gen_ref[:, cols])
        full = full[0:8] + full[8:16] - total * mean_ref[:, cols]
        for b in range(4):
            send_ref[at + b] = jnp.concatenate([cut(full, b), grams], axis=0).astype(BF16)
    rest = jnp.concatenate([jnp.zeros((pheno, LANE), F32), grams], axis=0).astype(BF16)
    for at in range(model_blocks, groups):
        send_ref[at] = rest


def next_kernel(got_ref, keep_ref, cols_ref, send_ref, coef_ref):
    groups = got_ref.shape[0]
    raw = jnp.sum(got_ref[...].astype(F32), axis=0)
    extra = raw[8:16]
    norm0, cross, square = [row_sum(extra[:, 3 * at : 3 * at + 3]) for at in range(3)]
    genetic, noise = cols_ref[0], cols_ref[1]
    rate = cross / norm0
    alpha0 = 1.0 / (rate + noise)
    norm1 = alpha0 * alpha0 * (square - rate * cross)
    on_image, on_start = -alpha0, alpha0 * rate + norm1 / norm0
    length = on_image * on_image * square + 2.0 * on_image * on_start * cross + on_start * on_start * norm0
    proj = on_image * (raw[0:8] * keep_ref[2]) + on_start * keep_ref[0]
    back = proj * keep_ref[2] * genetic
    energy = row_sum(proj * proj) * genetic
    lines = in_lanes([p.astype(F32)[:, 0:1] for p in split(energy, 3)])
    send = jnp.concatenate([back, lines], axis=0).astype(BF16)
    send_ref[...] = jnp.broadcast_to(send[None], (groups, 16, LANE))
    coef_ref[...] = in_lanes([x[:, 0:1] for x in (rate, alpha0, norm1, on_image, on_start, length)])


def back1_kernel(model_blocks, got_ref, gen_ref, mean_ref, send_ref):
    ways, pheno, _ = send_ref.shape
    rows = gen_ref.shape[0]
    width = rows // ways
    per = LANE // width
    shift = jnp.zeros((pheno, LANE), F32)
    extra = jnp.zeros((pheno, LANE), F32)
    for at in range(model_blocks):
        block = got_ref[at].astype(F32)
        shift = shift + block[0:8] * mean_ref[:, at * LANE : (at + 1) * LANE]
        extra = extra + block[8:16]
    energy = row_sum(extra)
    part = back_product(got_ref, gen_ref, model_blocks) - row_sum(shift)
    lane = iota((pheno, LANE), 1)
    for peer in range(ways):
        spot = (width * (peer % per) + width) % LANE
        send_ref[peer] = jnp.where(lane == spot, energy, cut(part, peer // per))


def finish_kernel(got_ref, start_ref, image_ref, coef_ref, cols_ref, out_ref, residual_ref):
    ways, pheno, _ = got_ref.shape
    rows = start_ref.shape[1]
    width = rows // ways
    per = LANE // width
    mine = lax.axis_index("var")
    tile, at = lax.div(mine, per), lax.rem(mine, per)
    got = jnp.sum(got_ref[...], axis=0)
    lane = iota((pheno, LANE), 1)
    curve = row_sum(jnp.where(lane == lax.rem(at * width + width, LANE), got, 0.0))
    start = jnp.zeros((pheno, LANE), F32)
    image = jnp.zeros((pheno, LANE), F32)
    for t in range(rows // LANE):
        start = jnp.where(tile == t, cut(start_ref[...], t), start)
        image = jnp.where(tile == t, cut(image_ref[...], t), image)
    coef, noise = coef_ref[...], cols_ref[1]
    rate, alpha0, norm1, on_image, on_start, length = [coef[:, i : i + 1] for i in range(6)]
    alpha1 = norm1 / (curve + noise * length)
    direction = on_image * image + on_start * start
    residual = -alpha0 * (image - rate * start) - alpha1 * (got + noise * direction)
    answer = alpha0 * start + alpha1 * direction
    out, left = answer[:, :width], residual[:, :width]
    for a in range(1, per):
        out = jnp.where(at == a, answer[:, a * width : (a + 1) * width], out)
        left = jnp.where(at == a, residual[:, a * width : (a + 1) * width], left)
    out_ref[...] = out
    residual_ref[...] = left


def exchange(x, axis):
    return lax.all_to_all(x, axis, 0, 0, tiled=True)


def shards(genotypes, imputed, centre, phenotypes, earlier, genetic, noise):
    rows, model = genotypes.shape
    other = imputed.shape[1]
    pheno = phenotypes.shape[0]
    groups, ways = lax.axis_size("samp"), lax.axis_size("var")
    model_blocks, other_blocks = model // LANE, other // LANE
    centre = centre[None, :]
    wide = (groups, 16, LANE)

    send, genotypes, cols = gather(groups, genotypes, imputed, centre, phenotypes, earlier, genetic, noise)
    got = exchange(send, "samp")
    owner = functools.partial(owner_kernel, float(rows * groups), model_blocks)
    send, keep = call(owner, [(wide, BF16, 0), ((4, pheno, LANE), F32, 0)], got, cols)
    got = exchange(send, "samp")
    back0 = functools.partial(back0_kernel, model_blocks, other_blocks)
    outs = [((ways, 16, rows // 2), BF16, 0), ((pheno, rows), F32, 0), ((1, model), F32, 0), ((pheno, other), F32, 1)]
    send, start, mean, scores = call(back0, outs, got, genotypes, centre, phenotypes, keep)
    got = exchange(send, "var")
    project = functools.partial(project_kernel, model_blocks)
    send, image = call(project, [(wide, BF16, 0), ((pheno, rows), F32, 0)], got, genotypes, start, mean)
    got = exchange(send, "samp")
    send, coef = call(next_kernel, [(wide, BF16, 0), ((pheno, LANE), F32, 0)], got, keep, cols)
    got = exchange(send, "samp")
    back1 = functools.partial(back1_kernel, model_blocks)
    (send,) = call(back1, [((ways, pheno, LANE), F32, 0)], got, genotypes, mean)
    got = exchange(send, "var")
    part = (pheno, rows // ways)
    out, residual = call(finish_kernel, [(part, F32, 1), (part, F32, 1)], got, start, image, coef, cols)
    return (out, residual, scores)


def solution(mesh):
    in_specs = (
        P("samp", "var"),
        P("samp", "var"),
        P("samp"),
        P(None, "samp"),
        P(None, "samp"),
        P(),
        P(),
    )
    out_specs = (P(None, ("samp", "var")), P(None, ("samp", "var")), P(None, "var"))
    return jax.shard_map(shards, mesh=mesh, in_specs=in_specs, out_specs=out_specs, check_vma=False)
```

time: 1120 us -> 108 us (0.10)
  blocking collectives: 600 us -> 99.4 us
  waiting for transfers between devices: 493 us -> 0 us
  between operations: 14.2 us -> 0.68 us
    psum x6 -> x0, blocking collectives: 600 us -> none  [the longest x3 296 us: inner(): return lax.psum((values[0],), 'samp')]
    psum x2 -> x0, waiting for transfers between devices: 493 us -> none  [operate(): summed_proj = lax.psum(partial_proj, 'samp')]
    all_to_all x0 -> x6, blocking collectives: none -> 99.4 us  [exchange(): return lax.all_to_all(x, axis, 0, 0, tiled=True)]
  transfers between devices with their start and end apart: 2 -> 0, of which waited for: 2 -> 0; matrix products, arithmetic and copies ran while one was open for 0% -> 0% of each run, Pallas kernels for 0% -> 0%
where the time goes in v2:
time: 108 us
  blocking collectives  99.4 us (92%)
  Pallas kernels  7.79 us (7%)
    all_to_all x6, blocking collectives, exchange(): return lax.all_to_all(x, axis, 0, 0, tiled=True)  99.4 us
    pallas_call x6, Pallas kernels, call(): pl.pallas_call(kernel, out_shape=[jax.ShapeDtypeStruct(shape, kind) if la...  4.16 us
    pallas_call x1, Pallas kernels, gather(): pl.pallas_call(gather_kernel, out_shape=[pltpu.VMEM((groups, 24, LANE), F...  3.63 us

profile of v2, /device:TPU:1, one launch (start us, length us, event | category | flops | bytes accessed | tf_op | source)
XLA Modules:
  0.0 107.9 jit_solution(13549003648062020294)
XLA Ops:
  0.6 0.0 copy-start
  0.6 0.0 copy-start.1
  0.7 3.6 %shard_map.94 = (f32[32,24,128]{2,1,0:T(8,128)S(1)}, bf16[512,2560]{1,0:T(8,128)(2,1)S(1)}, f32[2,8,128]{2,1,0:T(8,128)S(1)}) custom-call(bf16[512,2560]{1,0:T(8,128)(2,1)} %gen_hbm.1, bf16[512,1280]{1,0:T(8,128)(2,1)} %imp_hbm.1, s32[1,512]{1,0:T(1,128)} %bitcast.1, f32[8,512]{1,0:T(8,128)} %phen_ref.1, f32[8,512]{1,0:T(8,128)} %earl_hbm.1, f32[8]{0:T(128)} %genetic_hbm.1, ...), custom_call_target="tpu_custom_call" | custom-call | tf_op jit(solution)/shard_map/pallas_call | solution.py:140
  4.3 23.7 %all_to_all.30.got_ref = f32[32,24,128]{2,1,0:T(8,128)S(1)} all-to-all(f32[32,24,128]{2,1,0:T(8,128)S(1)} %get-tuple-element.18), channel_id=1, replica_groups=mesh['samp'=32,'var'=16] {'samp'}, dimensions={0} | all-to-all | bytes 786432 | tf_op jit(solution)/shard_map/all_to_all | solution.py:347
  28.0 0.3 shard_map.95
  28.2 12.1 %all_to_all.31.got_ref = bf16[32,16,128]{2,1,0:T(8,128)(2,1)S(1)} all-to-all(bf16[32,16,128]{2,1,0:T(8,128)(2,1)S(1)} %get-tuple-element.20), channel_id=1, replica_groups=mesh['samp'=32,'var'=16] {'samp'}, dimensions={0} | all-to-all | bytes 262144 | tf_op jit(solution)/shard_map/all_to_all | solution.py:347
  40.4 0.0 copy-done
  40.4 0.0 copy-done.1
  40.4 1.3 %shard_map.96 = (bf16[16,16,256]{2,1,0:T(8,128)(2,1)S(1)}, f32[8,512]{1,0:T(8,128)S(1)}, f32[1,2560]{1,0:T(1,128)S(1)}, f32[8,1280]{1,0:T(8,128)}) custom-call(bf16[32,16,128]{2,1,0:T(8,128)(2,1)S(1)} %all_to_all.31.got_ref, bf16[512,2560]{1,0:T(8,128)(2,1)S(1)} %get-tuple-element.21.gen_ref, s32[1,512]{1,0:T(1,128)S(1)} %bitcast.2, f32[8,512]{1,0:T(8,128)S(1)} %copy-done, ...), custom_call_target="tpu_custom_call" | custom-call | tf_op jit(solution)/shard_map/pallas_call | solution.py:162
  41.7 23.7 %all_to_all.32.got_ref = bf16[16,16,256]{2,1,0:T(8,128)(2,1)S(1)} all-to-all(bf16[16,16,256]{2,1,0:T(8,128)(2,1)S(1)} %get-tuple-element.23), channel_id=1, replica_groups=mesh['samp'=32,'var'=16] {'var'}, dimensions={0} | all-to-all | bytes 262144 | tf_op jit(solution)/shard_map/all_to_all | solution.py:347
  65.4 0.5 shard_map.97
  65.9 13.7 %all_to_all.33.got_ref = bf16[32,16,128]{2,1,0:T(8,128)(2,1)S(1)} all-to-all(bf16[32,16,128]{2,1,0:T(8,128)(2,1)S(1)} %get-tuple-element.26), channel_id=1, replica_groups=mesh['samp'=32,'var'=16] {'samp'}, dimensions={0} | all-to-all | bytes 262144 | tf_op jit(solution)/shard_map/all_to_all | solution.py:347
  79.6 0.4 shard_map.98
  79.9 12.1 %all_to_all.34.got_ref = bf16[32,16,128]{2,1,0:T(8,128)(2,1)S(1)} all-to-all(bf16[32,16,128]{2,1,0:T(8,128)(2,1)S(1)} %get-tuple-element.27), channel_id=1, replica_groups=mesh['samp'=32,'var'=16] {'samp'}, dimensions={0} | all-to-all | bytes 262144 | tf_op jit(solution)/shard_map/all_to_all | solution.py:347
  92.0 0.8 shard_map.99
  92.8 14.1 %all_to_all.35.got_ref = f32[16,8,128]{2,1,0:T(8,128)S(1)} all-to-all(f32[16,8,128]{2,1,0:T(8,128)S(1)} %shard_map.99), channel_id=1, replica_groups=mesh['samp'=32,'var'=16] {'var'}, dimensions={0} | all-to-all | bytes 131072 | tf_op jit(solution)/shard_map/all_to_all | solution.py:347
  106.9 1.0 shard_map.100
Async XLA Ops:
  0.6 39.7 %copy-start = (f32[8,512]{1,0:T(8,128)S(1)}, f32[8,512]{1,0:T(8,128)}, u32[]{:S(2)}) copy-start(f32[8,512]{1,0:T(8,128)} %phen_ref.1) | copy-start | bytes 49156
  0.6 39.7 %copy-start.1 = (s32[512]{0:T(512)S(1)}, s32[512]{0:T(512)}, u32[]{:S(2)}) copy-start(s32[512]{0:T(512)} %param.9) | copy-start | bytes 6148

commit v3 on v2

--- a/solution.py
+++ b/solution.py
@@ -14,6 +14,7 @@
 BASE = 4096.0
 STEPS = 5
 GRANT = 16 << 20
+NEAR, CORES = 4, 2
 BF16, F32 = jnp.bfloat16, jnp.float32
 NT = (((1,), (1,)), ((), ()))
 
@@ -53,6 +54,14 @@
 
 def cut(x, at):
     return x[:, at * LANE : (at + 1) * LANE]
+
+
+def square_sum(ref, first, wide):
+    acc = None
+    for at in range(0, ref.shape[0], 16):
+        part = ref[at : at + 16, first : first + wide]
+        acc = part * part if acc is None else acc + part * part
+    return jnp.sum(acc.astype(F32), axis=0, keepdims=True)
 
 
 def gather_kernel(
@@ -84,11 +93,9 @@
     pieces = [p.astype(F32) for p in split(phen_ref[...], 3)]
     phen = jnp.concatenate(pieces + [jnp.ones((pheno, rows), F32)], axis=0).astype(BF16)
     left = jnp.concatenate(pieces + [pairs], axis=0).astype(BF16)
-    left_square = jnp.where(slot == CENTRES - SLOTS, BASE, 0.0).astype(BF16)
     earl = earl_ref[...]
     pieces = [p.astype(F32) for p in split(earl, 3)]
     right = jnp.concatenate(pieces + [jnp.ones((pheno, rows), F32)], axis=0).astype(BF16)
-    right_square = jnp.ones((16, rows), BF16)
     sums = []
     for at in (0, 32, 64):
         full = dot_t(phen, jnp.where(spot == centre + at, 1.0, 0.0).astype(BF16))
@@ -113,17 +120,18 @@
         gen = gen_ref[:, step * wide : (step + 1) * wide]
         full = dot(left, gen)
         by_model = full[0:8] + full[8:16] + full[16:24]
-        packed = full[24:40] + dot(left_square, gen * gen)
+        packed, square = full[24:40], square_sum(gen_ref, step * wide, wide) * BASE
         for at in range(own):
             block = step * own + at
             out_ref[block, 0:8, :] = cut(by_model, at)
             out_ref[block, 8:16, :] = cut(packed[0:8], at)
-            out_ref[block, 16:24, :] = cut(packed[8:16], at) + table
+            counts = cut(packed[8:16], at) + table
+            out_ref[block, 16:24, :] = counts + jnp.where(row == CENTRES - SLOTS - 8, cut(square, at), 0.0)
         copies[6 + 2 * step].wait()
         imp = imp_ref[:, step * narrow : (step + 1) * narrow]
         full = dot(right, imp)
         by_other = full[0:8] + full[8:16] + full[16:24]
-        square = dot(right_square, imp * imp)[0:8]
+        square = square_sum(imp_ref, step * narrow, narrow)
         for at in range(other):
             block = first_other + step * other + at
             counts = jnp.where(row == 0, cut(full[24:32], at), jnp.where(row == 1, cut(square, at), table))
@@ -158,12 +166,10 @@
     )(*[pltpu.with_memory_space_constraint(x, pltpu.HBM) for x in operands])
 
 
-def call(kernel, outs, *operands):
+def call(kernel, outs, *operands, make=pltpu.VMEM):
     return pl.pallas_call(
         kernel,
-        out_shape=[
-            jax.ShapeDtypeStruct(shape, kind) if last else pltpu.VMEM(shape, kind) for shape, kind, last in outs
-        ],
+        out_shape=[make(shape, kind) for shape, kind in outs],
         in_specs=[pl.BlockSpec(memory_space=pltpu.VMEM)] * len(operands),
         out_specs=[pl.BlockSpec(memory_space=pltpu.VMEM)] * len(outs),
         compiler_params=pltpu.CompilerParams(vmem_limit_bytes=GRANT),
@@ -195,11 +201,13 @@
         seen = seen + line
         proj = proj - centre_mean[:, c : c + 1] * line
     mean = seen / total
-    scale = lax.rsqrt(high[CENTRES - SLOTS : CENTRES - SLOTS + 1] / total - mean * mean + 1e-05)
+    spread = high[CENTRES - SLOTS : CENTRES - SLOTS + 1] / total - mean * mean + 1e-05
+    scale = lax.rsqrt(spread)
     proj = (proj - left * mean) * scale
     back = proj * scale * cols_ref[0]
-    m0, m1, m2 = [x.astype(F32) for x in split(mean, 3)]
-    lines = jnp.where(row == 0, m0, jnp.where(row == 1, m1, jnp.where(row == 2, m2, 0.0)))
+    lines = jnp.zeros((pheno, LANE), F32)
+    for at, line in enumerate(split(mean, 3) + split(scale * scale, 3) + split(spread, 2)):
+        lines = jnp.where(row == at, line.astype(F32), lines)
 
     other_mean = raw[16:17] / total
     other_var = raw[17:18] / total - other_mean * other_mean + 1e-05
@@ -211,10 +219,7 @@
     owner = lax.axis_index("samp") < model_blocks
     send = jnp.concatenate([jnp.where(owner, back, score_top), jnp.where(owner, lines, score - score_top)], axis=0)
     send_ref[...] = jnp.broadcast_to(send.astype(BF16)[None], (groups, 16, LANE))
-    keep_ref[0] = proj
-    keep_ref[1] = jnp.broadcast_to(mean, (pheno, LANE))
-    keep_ref[2] = jnp.broadcast_to(scale, (pheno, LANE))
-    keep_ref[3] = centre_mean
+    keep_ref[...] = centre_mean
 
 
 def back_product(got_ref, gen_ref, model_blocks):
@@ -226,16 +231,32 @@
     return acc[0:8]
 
 
-def back0_kernel(model_blocks, other_blocks, got_ref, gen_ref, centre_ref, phen_ref, keep_ref, send_ref, start_ref, mean_ref, score_ref):
+def back0_kernel(
+    model_blocks, other_blocks,
+    got_ref, gen_ref, centre_ref, phen_ref, keep_ref, cols_ref,
+    send_ref, part_ref, start_ref, mean_ref, weight_ref, back_ref, score_ref, own_ref,
+):
     ways = send_ref.shape[0]
     pheno, rows = phen_ref.shape
     shift = jnp.zeros((pheno, LANE), F32)
+    own = jnp.zeros((pheno, LANE), F32)
     for at in range(model_blocks):
         block = got_ref[at].astype(F32)
+        cols = slice(at * LANE, (at + 1) * LANE)
         mean = block[8:9] + block[9:10] + block[10:11]
-        mean_ref[:, at * LANE : (at + 1) * LANE] = mean
+        mean_ref[:, cols] = mean
+        weight_ref[:, cols] = block[11:12] + block[12:13] + block[13:14]
+        back_ref[:, cols] = block[0:8]
         shift = shift + block[0:8] * mean
-    part = back_product(got_ref, gen_ref, model_blocks) - row_sum(shift)
+        own = own + block[0:8] * block[0:8] * (block[14:15] + block[15:16])
+    acc = None
+    for at in range(0, model_blocks, 2):
+        values = jnp.concatenate([got_ref[at], got_ref[at + 1]], axis=1)
+        part = dot_t(values, gen_ref[:, at * LANE : (at + 2) * LANE])
+        acc = part if acc is None else acc + part
+    part = acc[0:8] - row_sum(shift)
+    part_ref[...] = part
+    own_ref[...] = in_lanes([row_sum(own) / cols_ref[0][:, 0:1]])
     half = rows // 2
     send = jnp.concatenate([part[:, :half], part[:, half:]], axis=0).astype(BF16)
     send_ref[...] = jnp.broadcast_to(send[None], (ways, 16, half))
@@ -244,70 +265,90 @@
         score_ref[:, at * LANE : (at + 1) * LANE] = block[0:8] + block[8:16]
     centre = centre_ref[...]
     start = phen_ref[...]
-    centre_mean = keep_ref[3]
+    centre_mean = keep_ref[...]
     for c in range(CENTRES):
         start = start - jnp.where(centre == c, centre_mean[:, c : c + 1], 0.0)
     start_ref[...] = start
 
 
-def project_kernel(model_blocks, got_ref, gen_ref, start_ref, mean_ref, send_ref, image_ref):
-    groups = send_ref.shape[0]
-    pheno, rows = start_ref.shape
-    half = rows // 2
+def thirds(columns):
+    return in_lanes([p.astype(F32) for x in columns for p in split(x, 3)])
+
+
+def from_thirds(x, count):
+    return [row_sum(x[:, 3 * at : 3 * at + 3]) for at in range(count)]
+
+
+def project_kernel(got_ref, gen_ref, start_ref, mean_ref, send_ref, image_ref):
+    peers = send_ref.shape[0]
     both = jnp.sum(got_ref[...].astype(F32), axis=0)
     image = jnp.concatenate([both[0:8], both[8:16]], axis=1)
     image_ref[...] = image
     start = start_ref[...]
-    parts = []
-    for x in (start * start, start * image, image * image):
-        parts += [p.astype(F32) for p in split(row_sum(x), 3)]
-    grams = in_lanes(parts)
+    grams = thirds([row_sum(x) for x in (start * start, start * image, image * image)])
     total = row_sum(image)
     left = jnp.concatenate([p.astype(F32) for p in split(image, 2)], axis=0).astype(BF16)
-    for at in range(0, model_blocks, 4):
-        cols = slice(at * LANE, (at + 4) * LANE)
-        full = dot(left, gen_ref[:, cols])
-        full = full[0:8] + full[8:16] - total * mean_ref[:, cols]
-        for b in range(4):
-            send_ref[at + b] = jnp.concatenate([cut(full, b), grams], axis=0).astype(BF16)
-    rest = jnp.concatenate([jnp.zeros((pheno, LANE), F32), grams], axis=0).astype(BF16)
-    for at in range(model_blocks, groups):
-        send_ref[at] = rest
-
-
-def next_kernel(got_ref, keep_ref, cols_ref, send_ref, coef_ref):
-    groups = got_ref.shape[0]
-    raw = jnp.sum(got_ref[...].astype(F32), axis=0)
-    extra = raw[8:16]
-    norm0, cross, square = [row_sum(extra[:, 3 * at : 3 * at + 3]) for at in range(3)]
-    genetic, noise = cols_ref[0], cols_ref[1]
+    half = gen_ref.shape[1] // 2
+    for at in range(0, half, 2 * LANE):
+        parts = []
+        for first in (at, at + half):
+            cols = slice(first, first + 2 * LANE)
+            full = dot(left, gen_ref[:, cols])
+            parts.append(full[0:8] + full[8:16] - total * mean_ref[:, cols])
+        send = jnp.concatenate(parts, axis=0).astype(BF16)
+        for peer in range(peers):
+            send_ref[peer, :, at : at + 2 * LANE] = send
+    send = jnp.concatenate([grams, jnp.zeros_like(grams)], axis=0).astype(BF16)
+    for peer in range(peers):
+        send_ref[peer, :, half : half + LANE] = send
+
+
+def middle_kernel(got_ref, send_ref):
+    peers, _, wide = send_ref.shape
+    half = wide - LANE
+    got = jnp.sum(got_ref[...].astype(F32), axis=0)
+    grams = thirds(from_thirds(got[0:8, half:], 3))
+    tail = jnp.concatenate([grams, jnp.zeros_like(grams)], axis=0)
+    send = jnp.concatenate([got[:, :half], tail], axis=1).astype(BF16)
+    send_ref[...] = jnp.broadcast_to(send[None], send_ref.shape)
+
+
+def back1_kernel(
+    got_ref, gen_ref, mean_ref, weight_ref, back_ref, part_ref, own_ref, cols_ref, send_ref, coef_ref
+):
+    ways, pheno, _ = send_ref.shape
+    rows, model = gen_ref.shape
+    half = model // 2
+    wide = 2 * LANE
+    genetic, noise = cols_ref[0][:, 0:1], cols_ref[1][:, 0:1]
+    shift = jnp.zeros((pheno, wide), F32)
+    new = jnp.zeros((pheno, wide), F32)
+    mixed = jnp.zeros((pheno, wide), F32)
+    acc = None
+    for at in range(0, half, wide):
+        got = jnp.sum(got_ref[:, :, at : at + wide].astype(F32), axis=0)
+        for proj, first in ((got[0:8], at), (got[8:16], at + half)):
+            cols = slice(first, first + wide)
+            back = proj * weight_ref[:, cols] * genetic
+            new = new + proj * back
+            mixed = mixed + proj * back_ref[:, cols]
+            shift = shift + back * mean_ref[:, cols]
+            low = jnp.concatenate([p.astype(F32) for p in split(back, 2)], axis=0).astype(BF16)
+            part = dot_t(low, gen_ref[:, cols])
+            acc = part if acc is None else acc + part
+    grams = jnp.sum(got_ref[:, :, half:].astype(F32), axis=0)
+    norm0, cross, square = from_thirds(grams[0:8], 3)
     rate = cross / norm0
     alpha0 = 1.0 / (rate + noise)
     norm1 = alpha0 * alpha0 * (square - rate * cross)
     on_image, on_start = -alpha0, alpha0 * rate + norm1 / norm0
     length = on_image * on_image * square + 2.0 * on_image * on_start * cross + on_start * on_start * norm0
-    proj = on_image * (raw[0:8] * keep_ref[2]) + on_start * keep_ref[0]
-    back = proj * keep_ref[2] * genetic
-    energy = row_sum(proj * proj) * genetic
-    lines = in_lanes([p.astype(F32)[:, 0:1] for p in split(energy, 3)])
-    send = jnp.concatenate([back, lines], axis=0).astype(BF16)
-    send_ref[...] = jnp.broadcast_to(send[None], (groups, 16, LANE))
-    coef_ref[...] = in_lanes([x[:, 0:1] for x in (rate, alpha0, norm1, on_image, on_start, length)])
-
-
-def back1_kernel(model_blocks, got_ref, gen_ref, mean_ref, send_ref):
-    ways, pheno, _ = send_ref.shape
-    rows = gen_ref.shape[0]
+    coef_ref[...] = in_lanes([rate, alpha0, norm1, on_image, on_start, length])
+    part = on_image * (acc[0:8] + acc[8:16] - row_sum(shift)) + on_start * part_ref[...]
+    energy = on_image * on_image * row_sum(new) + on_start * on_start * own_ref[...][:, 0:1]
+    energy = energy + 2.0 * on_image * on_start * row_sum(mixed)
     width = rows // ways
     per = LANE // width
-    shift = jnp.zeros((pheno, LANE), F32)
-    extra = jnp.zeros((pheno, LANE), F32)
-    for at in range(model_blocks):
-        block = got_ref[at].astype(F32)
-        shift = shift + block[0:8] * mean_ref[:, at * LANE : (at + 1) * LANE]
-        extra = extra + block[8:16]
-    energy = row_sum(extra)
-    part = back_product(got_ref, gen_ref, model_blocks) - row_sum(shift)
     lane = iota((pheno, LANE), 1)
     for peer in range(ways):
         spot = (width * (peer % per) + width) % LANE
@@ -343,8 +384,8 @@
     residual_ref[...] = left
 
 
-def exchange(x, axis):
-    return lax.all_to_all(x, axis, 0, 0, tiled=True)
+def exchange(x, axis, sets=None):
+    return lax.all_to_all(x, axis, 0, 0, axis_index_groups=sets, tiled=True)
 
 
 def shards(genotypes, imputed, centre, phenotypes, earlier, genetic, noise):
@@ -354,27 +395,33 @@
     groups, ways = lax.axis_size("samp"), lax.axis_size("var")
     model_blocks, other_blocks = model // LANE, other // LANE
     centre = centre[None, :]
-    wide = (groups, 16, LANE)
+    along = groups // (NEAR * CORES)
+    at = lambda x, y, core: (x * NEAR + y) * CORES + core
+    planes = [[at(x, y, core) for x in range(along) for core in range(CORES)] for y in range(NEAR)]
+    lines = [[at(x, y, core) for y in range(NEAR)] for x in range(along) for core in range(CORES)]
+    half = (16, model // 2 + LANE)
 
     send, genotypes, cols = gather(groups, genotypes, imputed, centre, phenotypes, earlier, genetic, noise)
     got = exchange(send, "samp")
     owner = functools.partial(owner_kernel, float(rows * groups), model_blocks)
-    send, keep = call(owner, [(wide, BF16, 0), ((4, pheno, LANE), F32, 0)], got, cols)
+    send, keep = call(owner, [((groups, 16, LANE), BF16), ((pheno, LANE), F32)], got, cols)
     got = exchange(send, "samp")
     back0 = functools.partial(back0_kernel, model_blocks, other_blocks)
-    outs = [((ways, 16, rows // 2), BF16, 0), ((pheno, rows), F32, 0), ((1, model), F32, 0), ((pheno, other), F32, 1)]
-    send, start, mean, scores = call(back0, outs, got, genotypes, centre, phenotypes, keep)
+    row, wide = ((1, model), F32), ((pheno, rows), F32)
+    outs = [((ways, 16, rows // 2), BF16), wide, wide, row, row]
+    outs += [((pheno, model), F32), ((pheno, other), F32), ((pheno, LANE), F32)]
+    outs = call(back0, outs, got, genotypes, centre, phenotypes, keep, cols)
+    send, part, start, mean, weight, back, scores, own = outs
     got = exchange(send, "var")
-    project = functools.partial(project_kernel, model_blocks)
-    send, image = call(project, [(wide, BF16, 0), ((pheno, rows), F32, 0)], got, genotypes, start, mean)
-    got = exchange(send, "samp")
-    send, coef = call(next_kernel, [(wide, BF16, 0), ((pheno, LANE), F32, 0)], got, keep, cols)
-    got = exchange(send, "samp")
-    back1 = functools.partial(back1_kernel, model_blocks)
-    (send,) = call(back1, [((ways, pheno, LANE), F32, 0)], got, genotypes, mean)
+    outs = [((along * CORES,) + half, BF16), ((pheno, rows), F32)]
+    send, image = call(project_kernel, outs, got, genotypes, start, mean)
+    (send,) = call(middle_kernel, [((NEAR,) + half, BF16)], exchange(send, "samp", planes))
+    got = exchange(send, "samp", lines)
+    outs = [((ways, pheno, LANE), F32), ((pheno, LANE), F32)]
+    send, coef = call(back1_kernel, outs, got, genotypes, mean, weight, back, part, own, cols)
     got = exchange(send, "var")
-    part = (pheno, rows // ways)
-    out, residual = call(finish_kernel, [(part, F32, 1), (part, F32, 1)], got, start, image, coef, cols)
+    part = ((pheno, rows // ways), F32)
+    out, residual = call(finish_kernel, [part, part], got, start, image, coef, cols, make=jax.ShapeDtypeStruct)
     return (out, residual, scores)
 
 

time: 108 us -> 104 us (0.963); the launches traced: 108 us -> 102 us
  blocking collectives: 99.4 us -> 79.4 us
  waiting for transfers between devices: 0 us -> 10.9 us
  starting transfers between devices: 0 us -> 3.48 us
    all_to_all x6 -> x5, blocking collectives: 99.4 us -> 79.4 us  [exchange(): return lax.all_to_all(x, axis, 0, 0, axis_index_groups=sets, tiled=True)]
    all_to_all x0 -> x1, waiting for transfers between devices: none -> 10.9 us  [exchange(): return lax.all_to_all(x, axis, 0, 0, axis_index_groups=sets, tiled=True)]
    all_to_all x0 -> x1, starting transfers between devices: none -> 3.48 us  [exchange(): return lax.all_to_all(x, axis, 0, 0, axis_index_groups=sets, tiled=True)]
  transfers between devices with their start and end apart: 0 -> 1, of which waited for: 0 -> 1; matrix products, arithmetic and copies ran while one was open for 0% -> 1% of each run, Pallas kernels for 0% -> 0%
where the time goes in v3:
time: 104 us; the launch traced here: 102 us
  blocking collectives  79.4 us (76%)
  waiting for transfers between devices  10.9 us (10%)
  Pallas kernels  7.33 us (7%)
  starting transfers between devices  3.48 us (3%)
    all_to_all x5, blocking collectives, exchange(): return lax.all_to_all(x, axis, 0, 0, axis_index_groups=sets, tiled=True)  79.4 us
    all_to_all x1, waiting for transfers between devices, exchange(): return lax.all_to_all(x, axis, 0, 0, axis_index_groups=sets, tiled=True)  10.9 us
    pallas_call x6, Pallas kernels, call(): pl.pallas_call(kernel, out_shape=[make(shape, kind) for shape, kind in ou...  4.09 us
    all_to_all x1, starting transfers between devices, exchange(): return lax.all_to_all(x, axis, 0, 0, axis_index_groups=sets, tiled=True)  3.48 us
    pallas_call x1, Pallas kernels, gather(): pl.pallas_call(gather_kernel, out_shape=[pltpu.VMEM((groups, 24, LANE), F...  3.25 us
  transfers between devices with their start and end apart: 1, of which 1 were waited for; matrix products, arithmetic and copies ran while one was open for 1% of the time, Pallas kernels for 0%

profile of v3, /device:TPU:1, one launch (start us, length us, event | category | flops | bytes accessed | tf_op | source)
XLA Modules:
  0.0 102.4 jit_solution(18370785110068743874)
XLA Ops:
  0.6 0.0 copy-start
  0.6 0.0 copy-start.1
  0.7 3.2 %shard_map.94 = (f32[32,24,128]{2,1,0:T(8,128)S(1)}, bf16[512,2560]{1,0:T(8,128)(2,1)S(1)}, f32[2,8,128]{2,1,0:T(8,128)S(1)}) custom-call(bf16[512,2560]{1,0:T(8,128)(2,1)} %gen_hbm.1, bf16[512,1280]{1,0:T(8,128)(2,1)} %imp_hbm.1, s32[1,512]{1,0:T(1,128)} %bitcast.1, f32[8,512]{1,0:T(8,128)} %phen_ref.1, f32[8,512]{1,0:T(8,128)} %earl_hbm.1, f32[8]{0:T(128)} %genetic_hbm.1, ...), custom_call_target="tpu_custom_call" | custom-call | tf_op jit(solution)/shard_map/pallas_call | solution.py:148
  3.9 23.7 %all_to_all.30.got_ref = f32[32,24,128]{2,1,0:T(8,128)S(1)} all-to-all(f32[32,24,128]{2,1,0:T(8,128)S(1)} %get-tuple-element.22), channel_id=1, replica_groups=mesh['samp'=32,'var'=16] {'samp'}, dimensions={0} | all-to-all | bytes 786432 | tf_op jit(solution)/shard_map/all_to_all | solution.py:388
  27.6 0.3 shard_map.95
  27.8 12.1 %all_to_all.31.got_ref = bf16[32,16,128]{2,1,0:T(8,128)(2,1)S(1)} all-to-all(bf16[32,16,128]{2,1,0:T(8,128)(2,1)S(1)} %get-tuple-element.24), channel_id=1, replica_groups=mesh['samp'=32,'var'=16] {'samp'}, dimensions={0} | all-to-all | bytes 262144 | tf_op jit(solution)/shard_map/all_to_all | solution.py:388
  40.0 0.0 copy-done
  40.0 0.0 copy-done.1
  40.0 0.8 shard_map.96
  40.8 23.7 %all_to_all.32.got_ref = bf16[16,16,256]{2,1,0:T(8,128)(2,1)S(1)} all-to-all(bf16[16,16,256]{2,1,0:T(8,128)(2,1)S(1)} %get-tuple-element.27), channel_id=1, replica_groups=mesh['samp'=32,'var'=16] {'var'}, dimensions={0} | all-to-all | bytes 262144 | tf_op jit(solution)/shard_map/all_to_all | solution.py:388
  64.5 0.5 shard_map.97
  65.0 11.9 %all_to_all.33.got_ref = bf16[8,16,1408]{2,1,0:T(8,128)(2,1)S(1)} all-to-all(bf16[8,16,1408]{2,1,0:T(8,128)(2,1)S(1)} %get-tuple-element.30), channel_id=1, replica_groups={{0,16,128,144,256,272,384,400},{32,48,160,176,288,304,416,432},{64,80,1..., dimensions={0} | all-to-all | bytes 720896 | tf_op jit(solution)/shard_map/all_to_all | solution.py:388
  76.8 0.2 shard_map.98
  77.0 8.0 %all_to_all.34.got_ref = bf16[4,16,1408]{2,1,0:T(8,128)(2,1)S(1)} all-to-all(bf16[4,16,1408]{2,1,0:T(8,128)(2,1)S(1)} %shard_map.98), channel_id=1, replica_groups={{0,32,64,96},{16,48,80,112},{128,160,192,224},{144,176,208,240},{256,28..., dimensions={0} | all-to-all | bytes 360448 | tf_op jit(solution)/shard_map/all_to_all | solution.py:388
  85.0 1.4 %shard_map.99 = (f32[16,8,128]{2,1,0:T(8,128)}, f32[8,128]{1,0:T(8,128)S(1)}) custom-call(bf16[4,16,1408]{2,1,0:T(8,128)(2,1)S(1)} %all_to_all.34.got_ref, bf16[512,2560]{1,0:T(8,128)(2,1)S(1)} %get-tuple-element.25.gen_ref, f32[1,2560]{1,0:T(1,128)S(1)} %get-tuple-element.29.mean_ref, f32[1,2560]{1,0:T(1,128)S(1)} %get-tuple-element.31.weight_ref, ...), custom_call_target="tpu_custom_call" | custom-call | tf_op jit(solution)/shard_map/pallas_call | solution.py:170
  86.4 3.5 %all-to-all-start.5 = ((f32[16,8,128]{2,1,0:T(8,128)}), f32[16,8,128]{2,1,0:T(8,128)S(1)}, u32[]{:S(2)}, u32[]{:S(2)}) async-start(f32[16,8,128]{2,1,0:T(8,128)} %get-tuple-element.35), calls=%async_computation.5 | async-start | bytes 131072 | tf_op jit(solution)/shard_map/all_to_all | solution.py:388
  89.9 0.6 copy.10
  90.5 10.9 %all-to-all-done.5.got_ref = f32[16,8,128]{2,1,0:T(8,128)S(1)} async-done(((f32[16,8,128]{2,1,0:T(8,128)}), f32[16,8,128]{2,1,0:T(8,128)S(1)}, u32[]{:S(2)}, u32[]{:S(2)}) %all-to-all-start.5) | async-done | bytes 65568 | tf_op jit(solution)/shard_map/all_to_all | solution.py:388
  101.4 1.0 shard_map.100
Async XLA Ops:
  0.6 39.4 %copy-start = (f32[8,512]{1,0:T(8,128)S(1)}, f32[8,512]{1,0:T(8,128)}, u32[]{:S(2)}) copy-start(f32[8,512]{1,0:T(8,128)} %phen_ref.1) | copy-start | bytes 49156
  0.6 39.4 %copy-start.1 = (s32[512]{0:T(512)S(1)}, s32[512]{0:T(512)}, u32[]{:S(2)}) copy-start(s32[512]{0:T(512)} %param.9) | copy-start | bytes 6148
  86.4 15.0 %all-to-all-start.5 = ((f32[16,8,128]{2,1,0:T(8,128)}), f32[16,8,128]{2,1,0:T(8,128)S(1)}, u32[]{:S(2)}, u32[]{:S(2)}) async-start(f32[16,8,128]{2,1,0:T(8,128)} %get-tuple-element.35), calls=%async_computation.5 | async-start | bytes 131072 | tf_op jit(solution)/shard_map/all_to_all | solution.py:388

commit v4 on v3

--- a/solution.py
+++ b/solution.py
@@ -12,7 +12,7 @@
 SLOTS = 12
 LANE = 128
 BASE = 4096.0
-STEPS = 5
+STEPS = 2
 GRANT = 16 << 20
 NEAR, CORES = 4, 2
 BF16, F32 = jnp.bfloat16, jnp.float32
@@ -56,9 +56,9 @@
     return x[:, at * LANE : (at + 1) * LANE]
 
 
-def square_sum(ref, first, wide):
+def square_sum(ref, top, deep, first, wide):
     acc = None
-    for at in range(0, ref.shape[0], 16):
+    for at in range(top, top + deep, 16):
         part = ref[at : at + 16, first : first + wide]
         acc = part * part if acc is None else acc + part * part
     return jnp.sum(acc.astype(F32), axis=0, keepdims=True)
@@ -66,21 +66,20 @@
 
 def gather_kernel(
     gen_hbm, imp_hbm, centre_hbm, phen_hbm, earl_hbm, genetic_hbm, noise_hbm,
-    out_ref, gen_ref, cols_ref, imp_ref, centre_ref, phen_ref, earl_ref, scal_ref, sem,
+    out_ref, gen_ref, cols_ref, imp_ref, centre_ref, phen_ref, earl_ref, scal_ref, left_ref, right_ref, sem,
 ):
     rows, model = gen_ref.shape
     groups, pheno = out_ref.shape[0], phen_ref.shape[0]
-    wide, narrow = model // STEPS, imp_ref.shape[1] // STEPS
-    own, other = wide // LANE, narrow // LANE
-    first_other = own * STEPS
+    extra = imp_ref.shape[1]
+    deep, wide = rows // STEPS, 2 * LANE
+    model_blocks, other_blocks = model // LANE, extra // LANE
     small = [(centre_hbm, centre_ref), (phen_hbm, phen_ref), (earl_hbm, earl_ref)]
     small += [(genetic_hbm, scal_ref.at[0]), (noise_hbm, scal_ref.at[1])]
     copies = [pltpu.make_async_copy(x, y, sem.at[i]) for i, (x, y) in enumerate(small)]
     for step in range(STEPS):
-        cols = pl.ds(step * wide, wide)
-        copies.append(pltpu.make_async_copy(gen_hbm.at[:, cols], gen_ref.at[:, cols], sem.at[5 + 2 * step]))
-        cols = pl.ds(step * narrow, narrow)
-        copies.append(pltpu.make_async_copy(imp_hbm.at[:, cols], imp_ref.at[:, cols], sem.at[6 + 2 * step]))
+        part = pl.ds(step * deep, deep)
+        copies.append(pltpu.make_async_copy(gen_hbm.at[part], gen_ref.at[part], sem.at[5 + 2 * step]))
+        copies.append(pltpu.make_async_copy(imp_hbm.at[part], imp_ref.at[part], sem.at[6 + 2 * step]))
     for copy in copies:
         copy.start()
 
@@ -92,10 +91,10 @@
     pairs = jnp.where(slot < SLOTS, jnp.where(centre == slot, 1.0, jnp.where(centre == slot + SLOTS, BASE, 0.0)), 0.0)
     pieces = [p.astype(F32) for p in split(phen_ref[...], 3)]
     phen = jnp.concatenate(pieces + [jnp.ones((pheno, rows), F32)], axis=0).astype(BF16)
-    left = jnp.concatenate(pieces + [pairs], axis=0).astype(BF16)
+    left_ref[...] = jnp.concatenate(pieces + [pairs], axis=0).astype(BF16)
     earl = earl_ref[...]
     pieces = [p.astype(F32) for p in split(earl, 3)]
-    right = jnp.concatenate(pieces + [jnp.ones((pheno, rows), F32)], axis=0).astype(BF16)
+    right_ref[...] = jnp.concatenate(pieces + [jnp.ones((pheno, rows), F32)], axis=0).astype(BF16)
     sums = []
     for at in (0, 32, 64):
         full = dot_t(phen, jnp.where(spot == centre + at, 1.0, 0.0).astype(BF16))
@@ -103,7 +102,7 @@
     row = iota((pheno, LANE), 0)
     table = jnp.where(row < 4, 0.0, pltpu.roll(sums[0], 4, 0) + sums[1] + sums[2])
     moments = in_lanes([row_sum(earl), row_sum(earl * earl)])
-    for at in range(first_other + other * STEPS, groups):
+    for at in range(model_blocks + other_blocks, groups):
         out_ref[at, 0:8, :] = jnp.zeros((8, LANE), F32)
         out_ref[at, 8:16, :] = jnp.zeros((8, LANE), F32)
         out_ref[at, 16:24, :] = table
@@ -116,28 +115,42 @@
         cols_ref[at] = column * (1.0 / M) if at == 0 else column
 
     for step in range(STEPS):
+        top, last = step * deep, step == STEPS - 1
         copies[5 + 2 * step].wait()
-        gen = gen_ref[:, step * wide : (step + 1) * wide]
-        full = dot(left, gen)
-        by_model = full[0:8] + full[8:16] + full[16:24]
-        packed, square = full[24:40], square_sum(gen_ref, step * wide, wide) * BASE
-        for at in range(own):
-            block = step * own + at
-            out_ref[block, 0:8, :] = cut(by_model, at)
-            out_ref[block, 8:16, :] = cut(packed[0:8], at)
-            counts = cut(packed[8:16], at) + table
-            out_ref[block, 16:24, :] = counts + jnp.where(row == CENTRES - SLOTS - 8, cut(square, at), 0.0)
+        for first in range(0, model, wide):
+            cols = slice(first, first + wide)
+            full = dot(left_ref[:, top : top + deep], gen_ref[top : top + deep, cols])
+            square = square_sum(gen_ref, top, deep, first, wide) * BASE
+            by_model = full[0:8] + full[8:16] + full[16:24]
+            tail = full[32:40] + jnp.where(iota((pheno, wide), 0) == CENTRES - SLOTS - 8, square, 0.0)
+            for at in range(2):
+                block = first // LANE + at
+                for place, part in ((0, by_model), (8, full[24:32]), (16, tail)):
+                    part = cut(part, at)
+                    if step:
+                        part = part + out_ref[block, place : place + 8, :]
+                    if last and place == 16:
+                        part = part + table
+                    out_ref[block, place : place + 8, :] = part
         copies[6 + 2 * step].wait()
-        imp = imp_ref[:, step * narrow : (step + 1) * narrow]
-        full = dot(right, imp)
-        by_other = full[0:8] + full[8:16] + full[16:24]
-        square = square_sum(imp_ref, step * narrow, narrow)
-        for at in range(other):
-            block = first_other + step * other + at
-            counts = jnp.where(row == 0, cut(full[24:32], at), jnp.where(row == 1, cut(square, at), table))
-            out_ref[block, 0:8, :] = cut(by_other, at)
-            out_ref[block, 8:16, :] = moments
-            out_ref[block, 16:24, :] = counts
+        for first in range(0, extra, wide):
+            cols = slice(first, first + wide)
+            full = dot(right_ref[:, top : top + deep], imp_ref[top : top + deep, cols])
+            square = square_sum(imp_ref, top, deep, first, wide)
+            by_other = full[0:8] + full[8:16] + full[16:24]
+            lines = iota((pheno, wide), 0)
+            counts = jnp.where(lines == 0, full[24:32], jnp.where(lines == 1, square, 0.0))
+            for at in range(2):
+                block = model_blocks + first // LANE + at
+                for place, part in ((0, by_other), (16, counts)):
+                    part = cut(part, at)
+                    if step:
+                        part = part + out_ref[block, place : place + 8, :]
+                    if last and place == 16:
+                        part = part + table
+                    out_ref[block, place : place + 8, :] = part
+                if last:
+                    out_ref[block, 8:16, :] = moments
 
 
 def gather(groups, *operands):
@@ -160,18 +173,26 @@
             pltpu.VMEM((pheno, rows), F32),
             pltpu.VMEM((pheno, rows), F32),
             pltpu.SMEM((2, pheno), F32),
+            pltpu.VMEM((40, rows), BF16),
+            pltpu.VMEM((32, rows), BF16),
             pltpu.SemaphoreType.DMA((5 + 2 * STEPS,)),
         ],
         compiler_params=pltpu.CompilerParams(vmem_limit_bytes=GRANT),
     )(*[pltpu.with_memory_space_constraint(x, pltpu.HBM) for x in operands])
 
 
-def call(kernel, outs, *operands, make=pltpu.VMEM):
+def call(kernel, outs, *operands, make=pltpu.VMEM, out=None, scratch=()):
+    out_shape = [make(shape, kind) for shape, kind in outs]
+    out_specs = [pl.BlockSpec(memory_space=pltpu.VMEM)] * len(outs)
+    if out is not None:
+        out_shape.append(jax.ShapeDtypeStruct(*out))
+        out_specs.append(pl.BlockSpec(memory_space=pltpu.HBM))
     return pl.pallas_call(
         kernel,
-        out_shape=[make(shape, kind) for shape, kind in outs],
+        out_shape=out_shape,
         in_specs=[pl.BlockSpec(memory_space=pltpu.VMEM)] * len(operands),
-        out_specs=[pl.BlockSpec(memory_space=pltpu.VMEM)] * len(outs),
+        out_specs=out_specs,
+        scratch_shapes=scratch,
         compiler_params=pltpu.CompilerParams(vmem_limit_bytes=GRANT),
     )(*[pltpu.with_memory_space_constraint(x, pltpu.VMEM) for x in operands])
 
@@ -314,8 +335,11 @@
 
 
 def back1_kernel(
-    got_ref, gen_ref, mean_ref, weight_ref, back_ref, part_ref, own_ref, cols_ref, send_ref, coef_ref
+    got_ref, gen_ref, mean_ref, weight_ref, back_ref, part_ref, own_ref, cols_ref, score_ref,
+    send_ref, coef_ref, out_hbm, sem,
 ):
+    copy = pltpu.make_async_copy(score_ref, out_hbm, sem)
+    copy.start()
     ways, pheno, _ = send_ref.shape
     rows, model = gen_ref.shape
     half = model // 2
@@ -353,6 +377,7 @@
     for peer in range(ways):
         spot = (width * (peer % per) + width) % LANE
         send_ref[peer] = jnp.where(lane == spot, energy, cut(part, peer // per))
+    copy.wait()
 
 
 def finish_kernel(got_ref, start_ref, image_ref, coef_ref, cols_ref, out_ref, residual_ref):
@@ -418,7 +443,9 @@
     (send,) = call(middle_kernel, [((NEAR,) + half, BF16)], exchange(send, "samp", planes))
     got = exchange(send, "samp", lines)
     outs = [((ways, pheno, LANE), F32), ((pheno, LANE), F32)]
-    send, coef = call(back1_kernel, outs, got, genotypes, mean, weight, back, part, own, cols)
+    kept = (got, genotypes, mean, weight, back, part, own, cols, scores)
+    out, sem = ((pheno, other), F32), (pltpu.SemaphoreType.DMA,)
+    send, coef, scores = call(back1_kernel, outs, *kept, out=out, scratch=sem)
     got = exchange(send, "var")
     part = ((pheno, rows // ways), F32)
     out, residual = call(finish_kernel, [part, part], got, start, image, coef, cols, make=jax.ShapeDtypeStruct)

time: 104 us -> 102 us (0.981)
  blocking collectives: 79.4 us -> 93.5 us
  waiting for transfers between devices: 10.9 us -> 0 us
  starting transfers between devices: 3.48 us -> 0 us
  Pallas kernels: 7.33 us -> 6.13 us
    all_to_all x5 -> x6, blocking collectives: 79.4 us -> 93.5 us  [exchange(): return lax.all_to_all(x, axis, 0, 0, axis_index_groups=sets, tiled=True)]
    all_to_all x1 -> x0, waiting for transfers between devices: 10.9 us -> none  [exchange(): return lax.all_to_all(x, axis, 0, 0, axis_index_groups=sets, tiled=True)]
    all_to_all x1 -> x0, starting transfers between devices: 3.48 us -> none  [exchange(): return lax.all_to_all(x, axis, 0, 0, axis_index_groups=sets, tiled=True)]
  transfers between devices with their start and end apart: 1 -> 0, of which waited for: 1 -> 0; matrix products, arithmetic and copies ran while one was open for 1% -> 0% of each run, Pallas kernels for 0% -> 0%
where the time goes in v4:
time: 102 us; the launch traced here: 100 us
  blocking collectives  93.5 us (92%)
  Pallas kernels  6.13 us (6%)
    all_to_all x6, blocking collectives, exchange(): return lax.all_to_all(x, axis, 0, 0, axis_index_groups=sets, tiled=True)  93.5 us
    pallas_call x6, Pallas kernels, call(): pl.pallas_call(kernel, out_shape=out_shape, in_specs=[pl.BlockSpec(memory...  3.48 us
    pallas_call x1, Pallas kernels, gather(): pl.pallas_call(gather_kernel, out_shape=[pltpu.VMEM((groups, 24, LANE), F...  2.65 us

profile of v4, /device:TPU:1, one launch (start us, length us, event | category | flops | bytes accessed | tf_op | source)
XLA Modules:
  0.0 100.3 jit_solution(18308506082607035688)
XLA Ops:
  0.6 0.0 copy-start
  0.6 0.0 copy-start.1
  0.7 2.7 %shard_map.94 = (f32[32,24,128]{2,1,0:T(8,128)S(1)}, bf16[512,2560]{1,0:T(8,128)(2,1)S(1)}, f32[2,8,128]{2,1,0:T(8,128)S(1)}) custom-call(bf16[512,2560]{1,0:T(8,128)(2,1)} %gen_hbm.1, bf16[512,1280]{1,0:T(8,128)(2,1)} %imp_hbm.1, s32[1,512]{1,0:T(1,128)} %bitcast.1, f32[8,512]{1,0:T(8,128)} %phen_ref.1, f32[8,512]{1,0:T(8,128)} %earl_hbm.1, f32[8]{0:T(128)} %genetic_hbm.1, ...), custom_call_target="tpu_custom_call" | custom-call | tf_op jit(solution)/shard_map/pallas_call | solution.py:161
  3.3 23.7 %all_to_all.30.got_ref = f32[32,24,128]{2,1,0:T(8,128)S(1)} all-to-all(f32[32,24,128]{2,1,0:T(8,128)S(1)} %get-tuple-element.23), channel_id=1, replica_groups=mesh['samp'=32,'var'=16] {'samp'}, dimensions={0} | all-to-all | bytes 786432 | tf_op jit(solution)/shard_map/all_to_all | solution.py:413
  27.0 0.3 shard_map.95
  27.2 12.1 %all_to_all.31.got_ref = bf16[32,16,128]{2,1,0:T(8,128)(2,1)S(1)} all-to-all(bf16[32,16,128]{2,1,0:T(8,128)(2,1)S(1)} %get-tuple-element.25), channel_id=1, replica_groups=mesh['samp'=32,'var'=16] {'samp'}, dimensions={0} | all-to-all | bytes 262144 | tf_op jit(solution)/shard_map/all_to_all | solution.py:413
  39.4 0.0 copy-done
  39.4 0.0 copy-done.1
  39.4 0.8 shard_map.96
  40.2 23.7 %all_to_all.32.got_ref = bf16[16,16,256]{2,1,0:T(8,128)(2,1)S(1)} all-to-all(bf16[16,16,256]{2,1,0:T(8,128)(2,1)S(1)} %get-tuple-element.28), channel_id=1, replica_groups=mesh['samp'=32,'var'=16] {'var'}, dimensions={0} | all-to-all | bytes 262144 | tf_op jit(solution)/shard_map/all_to_all | solution.py:413
  63.9 0.5 shard_map.97
  64.4 11.9 %all_to_all.33.got_ref = bf16[8,16,1408]{2,1,0:T(8,128)(2,1)S(1)} all-to-all(bf16[8,16,1408]{2,1,0:T(8,128)(2,1)S(1)} %get-tuple-element.31), channel_id=1, replica_groups={{0,16,128,144,256,272,384,400},{32,48,160,176,288,304,416,432},{64,80,1..., dimensions={0} | all-to-all | bytes 720896 | tf_op jit(solution)/shard_map/all_to_all | solution.py:413
  76.2 0.2 shard_map.98
  76.4 8.0 %all_to_all.34.got_ref = bf16[4,16,1408]{2,1,0:T(8,128)(2,1)S(1)} all-to-all(bf16[4,16,1408]{2,1,0:T(8,128)(2,1)S(1)} %shard_map.98), channel_id=1, replica_groups={{0,32,64,96},{16,48,80,112},{128,160,192,224},{144,176,208,240},{256,28..., dimensions={0} | all-to-all | bytes 360448 | tf_op jit(solution)/shard_map/all_to_all | solution.py:413
  84.4 0.8 shard_map.99
  85.2 14.1 %all_to_all.35.got_ref = f32[16,8,128]{2,1,0:T(8,128)S(1)} all-to-all(f32[16,8,128]{2,1,0:T(8,128)S(1)} %get-tuple-element.37), channel_id=1, replica_groups=mesh['samp'=32,'var'=16] {'var'}, dimensions={0} | all-to-all | bytes 131072 | tf_op jit(solution)/shard_map/all_to_all | solution.py:413
  99.3 1.0 shard_map.100
Async XLA Ops:
  0.6 38.8 %copy-start = (f32[8,512]{1,0:T(8,128)S(1)}, f32[8,512]{1,0:T(8,128)}, u32[]{:S(2)}) copy-start(f32[8,512]{1,0:T(8,128)} %phen_ref.1) | copy-start | bytes 49156
  0.6 38.8 %copy-start.1 = (s32[512]{0:T(512)S(1)}, s32[512]{0:T(512)}, u32[]{:S(2)}) copy-start(s32[512]{0:T(512)} %param.9) | copy-start | bytes 6148

commit v5 on v4

v5 whole, which is shorter than its diff:
```python
import functools

import jax
import jax.numpy as jnp
from jax import lax
from jax.experimental import pallas as pl
from jax.experimental.pallas import tpu as pltpu
from jax.sharding import PartitionSpec as P

M = 40960
CENTRES = 22
SLOTS = 12
LANE = 128
BASE = 4096.0
STEPS = 2
GRANT = 16 << 20
NEAR, CORES = 4, 2
BF16, F32 = jnp.bfloat16, jnp.float32
NT = (((1,), (1,)), ((), ()))


def split(x, parts):
    out = []
    for _ in range(parts):
        top = x.astype(BF16)
        out.append(top)
        x = x - top.astype(F32)
    return out


def dot(x, y):
    return jnp.dot(x, y, preferred_element_type=F32)


def dot_t(x, y):
    return lax.dot_general(x, y, NT, preferred_element_type=F32)


def iota(shape, dim):
    return lax.broadcasted_iota(jnp.int32, shape, dim)


def row_sum(x):
    return jnp.sum(x, axis=1, keepdims=True)


def in_lanes(columns):
    lane = iota((columns[0].shape[0], LANE), 1)
    out = jnp.zeros((columns[0].shape[0], LANE), F32)
    for at, column in enumerate(columns):
        out = jnp.where(lane == at, column, out)
    return out


def cut(x, at):
    return x[:, at * LANE : (at + 1) * LANE]


def square_sum(ref, top, deep, first, wide):
    acc = None
    for at in range(top, top + deep, 16):
        part = ref[at : at + 16, first : first + wide]
        acc = part * part if acc is None else acc + part * part
    return jnp.sum(acc.astype(F32), axis=0, keepdims=True)


def gather_kernel(
    gen_hbm, imp_hbm, centre_hbm, phen_hbm, earl_hbm, genetic_hbm, noise_hbm,
    out_ref, gen_ref, cols_ref, imp_ref, centre_ref, phen_ref, earl_ref, scal_ref, left_ref, right_ref, model_ref, other_ref, sem,
):
    rows, model = gen_ref.shape
    groups, pheno = out_ref.shape[0], phen_ref.shape[0]
    extra = imp_ref.shape[1]
    deep, wide = rows // STEPS, 2 * LANE
    span, side = model // groups, extra // groups
    small = [(centre_hbm, centre_ref), (phen_hbm, phen_ref), (earl_hbm, earl_ref)]
    small += [(genetic_hbm, scal_ref.at[0]), (noise_hbm, scal_ref.at[1])]
    copies = [pltpu.make_async_copy(x, y, sem.at[i]) for i, (x, y) in enumerate(small)]
    for step in range(STEPS):
        part = pl.ds(step * deep, deep)
        copies.append(pltpu.make_async_copy(gen_hbm.at[part], gen_ref.at[part], sem.at[5 + 2 * step]))
        copies.append(pltpu.make_async_copy(imp_hbm.at[part], imp_ref.at[part], sem.at[6 + 2 * step]))
    for copy in copies:
        copy.start()

    spot = iota((LANE, rows), 0)
    slot = iota((16, rows), 0)
    for copy in copies[:3]:
        copy.wait()
    centre = centre_ref[...]
    pairs = jnp.where(slot < SLOTS, jnp.where(centre == slot, 1.0, jnp.where(centre == slot + SLOTS, BASE, 0.0)), 0.0)
    pieces = [p.astype(F32) for p in split(phen_ref[...], 3)]
    phen = jnp.concatenate(pieces + [jnp.ones((pheno, rows), F32)], axis=0).astype(BF16)
    left_ref[...] = jnp.concatenate(pieces + [pairs], axis=0).astype(BF16)
    earl = earl_ref[...]
    pieces = [p.astype(F32) for p in split(earl, 3)]
    right_ref[...] = jnp.concatenate(pieces + [jnp.ones((pheno, rows), F32)], axis=0).astype(BF16)
    sums = []
    here = jnp.where(spot == centre, 1.0, 0.0).astype(BF16)
    full = dot_t(phen, here)
    row, lane = iota((pheno, LANE), 0), iota((pheno, LANE), 1)
    sums, count = full[0:8] + full[8:16] + full[16:24], full[24:32]
    own_mean = sums / jnp.maximum(count, 1.0)
    full = dot(jnp.concatenate([p.astype(F32) for p in split(own_mean, 3)], axis=0).astype(BF16), here)
    apart = phen_ref[...] - (full[0:8] + full[8:16] + full[16:24])
    within = row_sum(apart * apart)
    table = pltpu.roll(sums, span, 1) + pltpu.roll(count, span + CENTRES, 1)
    table = table + pltpu.roll(in_lanes([within, row_sum(earl), row_sum(earl * earl)]), span + 2 * CENTRES, 1)
    for copy in copies[3:5]:
        copy.wait()
    for at in range(2):
        column = jnp.zeros((pheno, LANE), F32)
        for k in range(pheno):
            column = jnp.where(row == k, scal_ref[at, k], column)
        cols_ref[at] = column * (1.0 / M) if at == 0 else column

    for step in range(STEPS):
        top, last = step * deep, step == STEPS - 1
        copies[5 + 2 * step].wait()
        for first in range(0, model, wide):
            cols = slice(first, first + wide)
            full = dot(left_ref[:, top : top + deep], gen_ref[top : top + deep, cols])
            square = square_sum(gen_ref, top, deep, first, wide) * BASE
            tail = full[32:40] + jnp.where(iota((pheno, wide), 0) == CENTRES - SLOTS - 8, square, 0.0)
            for place, part in ((0, full[0:8] + full[8:16] + full[16:24]), (8, full[24:32]), (16, tail)):
                model_ref[place : place + 8, cols] = part + model_ref[place : place + 8, cols] if step else part
        copies[6 + 2 * step].wait()
        for first in range(0, extra, wide):
            cols = slice(first, first + wide)
            full = dot(right_ref[:, top : top + deep], imp_ref[top : top + deep, cols])
            square = square_sum(imp_ref, top, deep, first, wide)
            lines = iota((pheno, wide), 0)
            counts = jnp.where(lines == 0, full[24:32], jnp.where(lines == 1, square, 0.0))
            for place, part in ((0, full[0:8] + full[8:16] + full[16:24]), (8, counts)):
                other_ref[place : place + 8, cols] = part + other_ref[place : place + 8, cols] if step else part

    def window(ref, place, first, width, to):
        block, skip = divmod(first, LANE)
        turn = (to - skip) % LANE
        out = pltpu.roll(ref[place : place + 8, block * LANE : (block + 1) * LANE], turn, 1)
        if skip + width > LANE:
            more = pltpu.roll(ref[place : place + 8, (block + 1) * LANE : (block + 2) * LANE], turn, 1)
            out = jnp.where(lane < to + LANE - skip, out, more)
        return out

    for at in range(groups):
        mine = lambda place: window(model_ref, place, at * span, span, 0)
        more = lambda place: jnp.where(lane < span + side, window(other_ref, place, at * side, side, span), 0.0)
        top = jnp.where(lane < span, mine(0), more(0))
        centre_rows = jnp.where(lane < span, mine(8), table)
        tail = jnp.where(lane < span, mine(16), more(8))
        for place, part in enumerate((top[0:4], top[4:8], centre_rows[0:4], centre_rows[4:8], tail[0:4])):
            out_ref[at, :, place * LANE : (place + 1) * LANE] = part


def gather(groups, *operands):
    genotypes, imputed, _, phenotypes = operands[:4]
    rows, model = genotypes.shape
    other = imputed.shape[1]
    pheno = phenotypes.shape[0]
    return pl.pallas_call(
        gather_kernel,
        out_shape=[
            pltpu.VMEM((groups, 4, 5 * LANE), F32),
            pltpu.VMEM((rows, model), BF16),
            pltpu.VMEM((2, pheno, LANE), F32),
        ],
        in_specs=[pl.BlockSpec(memory_space=pltpu.HBM)] * len(operands),
        out_specs=[pl.BlockSpec(memory_space=pltpu.VMEM)] * 3,
        scratch_shapes=[
            pltpu.VMEM((rows, other), BF16),
            pltpu.VMEM((1, rows), jnp.int32),
            pltpu.VMEM((pheno, rows), F32),
            pltpu.VMEM((pheno, rows), F32),
            pltpu.SMEM((2, pheno), F32),
            pltpu.VMEM((40, rows), BF16),
            pltpu.VMEM((32, rows), BF16),
            pltpu.VMEM((24, model), F32),
            pltpu.VMEM((16, other), F32),
            pltpu.SemaphoreType.DMA((5 + 2 * STEPS,)),
        ],
        compiler_params=pltpu.CompilerParams(vmem_limit_bytes=GRANT),
    )(*[pltpu.with_memory_space_constraint(x, pltpu.HBM) for x in operands])


def call(kernel, outs, *operands, make=pltpu.VMEM, out=None, scratch=()):
    out_shape = [make(shape, kind) for shape, kind in outs]
    out_specs = [pl.BlockSpec(memory_space=pltpu.VMEM)] * len(outs)
    if out is not None:
        out_shape.append(jax.ShapeDtypeStruct(*out))
        out_specs.append(pl.BlockSpec(memory_space=pltpu.HBM))
    return pl.pallas_call(
        kernel,
        out_shape=out_shape,
        in_specs=[pl.BlockSpec(memory_space=pltpu.VMEM)] * len(operands),
        out_specs=out_specs,
        scratch_shapes=scratch,
        compiler_params=pltpu.CompilerParams(vmem_limit_bytes=GRANT),
    )(*[pltpu.with_memory_space_constraint(x, pltpu.VMEM) for x in operands])


def owner_kernel(total, span, side, got_ref, cols_ref, send_ref, keep_ref, norm_ref):
    groups, pheno = got_ref.shape[0], 8
    row, lane = iota((pheno, LANE), 0), iota((pheno, LANE), 1)
    pieces = [got_ref[:, :, at * LANE : (at + 1) * LANE] for at in range(5)]
    raw = [jnp.sum(x, axis=0) for x in pieces]
    tops = [jnp.floor(x * (1.0 / BASE)) for x in pieces[2:]]
    low = jnp.concatenate([jnp.sum(x - BASE * y, axis=0) for x, y in zip(pieces[2:], tops)], axis=0)
    high = jnp.concatenate([jnp.sum(y, axis=0) for y in tops], axis=0)
    product = jnp.concatenate(raw[0:2], axis=0)
    table = jnp.concatenate(raw[2:4], axis=0)
    sums = jnp.where(lane < CENTRES, pltpu.roll(table, LANE - span, 1), 0.0)
    count = jnp.where(lane < CENTRES, pltpu.roll(table, LANE - span - CENTRES, 1), 0.0)
    centre_mean = sums / jnp.maximum(count, 1.0)
    left = row_sum(sums - centre_mean * count)
    extra = span + 2 * CENTRES
    within, first, second = [table[:, extra + at : extra + at + 1] for at in range(3)]

    proj = product
    seen = jnp.zeros((1, LANE), F32)
    for c in range(CENTRES):
        line = low[c : c + 1] if c < SLOTS else high[c - SLOTS : c - SLOTS + 1]
        seen = seen + line
        proj = proj - centre_mean[:, c : c + 1] * line
    mean = seen / total
    spread = high[CENTRES - SLOTS : CENTRES - SLOTS + 1] / total - mean * mean + 1e-05
    scale = lax.rsqrt(spread)
    proj = (proj - left * mean) * scale
    back = proj * scale * cols_ref[0]
    lines = jnp.zeros((pheno, LANE), F32)
    for at, line in enumerate(split(mean, 3) + split(scale * scale, 3) + split(spread, 2)):
        lines = jnp.where(row == at, line.astype(F32), lines)

    other_mean = raw[4][0:1] / total
    other_var = raw[4][1:2] / total - other_mean * other_mean + 1e-05
    earlier_var = second / total + 1e-05
    score = (product - first * other_mean) / jnp.sqrt(total * other_var * earlier_var)
    score_top = score.astype(BF16).astype(F32)

    here, there = lane < span, lane < span + side
    top = jnp.where(here, back, jnp.where(there, score_top, 0.0))
    rest = jnp.where(here, lines, jnp.where(there, score - score_top, 0.0))
    send = jnp.concatenate([top, rest], axis=0).astype(BF16)
    send_ref[...] = jnp.broadcast_to(send[None], (groups, 16, LANE))
    keep_ref[...] = centre_mean

    middle = pltpu.roll(centre_mean, span, 1)
    halves = []
    for half in range(2):
        between = jnp.zeros((pheno // 2, LANE), F32)
        for at in range(groups):
            part = got_ref[at, :, (2 + half) * LANE : (3 + half) * LANE]
            counted = pltpu.roll(part, LANE - CENTRES, 1)
            apart = part - counted * middle[4 * half : 4 * half + 4]
            between = between + apart * apart / jnp.maximum(counted, 1.0)
        halves.append(between)
    between = jnp.concatenate(halves, axis=0)
    between = jnp.where((lane >= span) & (lane < span + CENTRES), between, 0.0)
    norm_ref[...] = jnp.broadcast_to(row_sum(between) + within, (pheno, LANE))


def back0_kernel(
    span, side, got_ref, gen_ref, centre_ref, phen_ref, keep_ref, cols_ref,
    send_ref, start_ref, mean_ref, weight_ref, back_ref, score_ref, own_ref,
):
    ways = send_ref.shape[0]
    pheno, rows = phen_ref.shape
    model, other = gen_ref.shape[1], score_ref.shape[1]

    def block_of(at, width, skip, rows, load):
        lane = iota((rows, LANE), 1)
        out = None
        for owner in range(at * LANE // width, ((at + 1) * LANE - 1) // width + 1):
            first = owner * width - at * LANE
            part = pltpu.roll(load(owner), (first - skip) % LANE, 1)
            out = part if out is None else jnp.where(lane < first, out, part)
        return out

    shift = jnp.zeros((pheno, LANE), F32)
    own = jnp.zeros((pheno, LANE), F32)
    acc = None
    for pair in range(0, model // LANE, 2):
        values = []
        for at in (pair, pair + 1):
            block = block_of(at, span, 0, 16, lambda owner: got_ref[owner].astype(F32))
            cols = slice(at * LANE, (at + 1) * LANE)
            mean = block[8:9] + block[9:10] + block[10:11]
            mean_ref[:, cols] = mean
            weight_ref[:, cols] = block[11:12] + block[12:13] + block[13:14]
            back_ref[:, cols] = block[0:8]
            shift = shift + block[0:8] * mean
            own = own + block[0:8] * block[0:8] * (block[14:15] + block[15:16])
            values.append(block.astype(BF16))
        part = dot_t(jnp.concatenate(values, axis=1), gen_ref[:, pair * LANE : (pair + 2) * LANE])
        acc = part if acc is None else acc + part
    part = acc[0:8] - row_sum(shift)
    own_ref[...] = in_lanes([row_sum(own) / cols_ref[0][:, 0:1]])
    half = rows // 2
    send = jnp.concatenate([part[:, :half], part[:, half:]], axis=0).astype(BF16)
    send_ref[...] = jnp.broadcast_to(send[None], (ways, 16, half))
    for at in range(other // LANE):
        load = lambda owner: got_ref[owner].astype(F32)[0:8] + got_ref[owner].astype(F32)[8:16]
        score_ref[:, at * LANE : (at + 1) * LANE] = block_of(at, side, span, pheno, load)
    centre = centre_ref[...]
    start = phen_ref[...]
    centre_mean = keep_ref[...]
    for c in range(CENTRES):
        start = start - jnp.where(centre == c, centre_mean[:, c : c + 1], 0.0)
    start_ref[...] = start


def project_kernel(got_ref, gen_ref, mean_ref, send_ref, image_ref):
    peers = send_ref.shape[0]
    both = jnp.sum(got_ref[...].astype(F32), axis=0)
    image = jnp.concatenate([both[0:8], both[8:16]], axis=1)
    image_ref[...] = image
    total = row_sum(image)
    left = jnp.concatenate([p.astype(F32) for p in split(image, 2)], axis=0).astype(BF16)
    half = gen_ref.shape[1] // 2
    for at in range(0, half, 2 * LANE):
        parts = []
        for first in (at, at + half):
            cols = slice(first, first + 2 * LANE)
            full = dot(left, gen_ref[:, cols])
            parts.append(full[0:8] + full[8:16] - total * mean_ref[:, cols])
        send = jnp.concatenate(parts, axis=0).astype(BF16)
        for peer in range(peers):
            send_ref[peer, :, at : at + 2 * LANE] = send


def middle_kernel(got_ref, send_ref):
    got = jnp.sum(got_ref[...].astype(F32), axis=0)
    send_ref[...] = jnp.broadcast_to(got.astype(BF16)[None], send_ref.shape)


def back1_kernel(
    got_ref, gen_ref, mean_ref, weight_ref, back_ref, own_ref, cols_ref, score_ref, send_ref, out_hbm, sem
):
    copy = pltpu.make_async_copy(score_ref, out_hbm, sem)
    copy.start()
    ways, pheno, _ = send_ref.shape
    rows, model = gen_ref.shape
    half = model // 2
    wide = 2 * LANE
    genetic = cols_ref[0][:, 0:1]
    shift = jnp.zeros((pheno, wide), F32)
    new = jnp.zeros((pheno, wide), F32)
    mixed = jnp.zeros((pheno, wide), F32)
    acc = None
    for at in range(0, half, wide):
        got = jnp.sum(got_ref[:, :, at : at + wide].astype(F32), axis=0)
        for proj, first in ((got[0:8], at), (got[8:16], at + half)):
            cols = slice(first, first + wide)
            back = proj * weight_ref[:, cols] * genetic
            new = new + proj * back
            mixed = mixed + proj * back_ref[:, cols]
            shift = shift + back * mean_ref[:, cols]
            low = jnp.concatenate([p.astype(F32) for p in split(back, 2)], axis=0).astype(BF16)
            part = dot_t(low, gen_ref[:, cols])
            acc = part if acc is None else acc + part
    part = acc[0:8] + acc[8:16] - row_sum(shift)
    energies = (own_ref[...][:, 0:1], row_sum(mixed), row_sum(new))
    width = rows // ways
    per = LANE // width
    lane = iota((pheno, LANE), 1)
    for peer in range(ways):
        send = cut(part, peer // per)
        for at, energy in enumerate(energies):
            send = jnp.where(lane == (width * (peer % per) + width + at) % LANE, energy, send)
        send_ref[peer] = send
    copy.wait()


def finish_kernel(got_ref, start_ref, image_ref, norm_ref, cols_ref, out_ref, residual_ref):
    ways, pheno, _ = got_ref.shape
    rows = start_ref.shape[1]
    width = rows // ways
    per = LANE // width
    mine = lax.axis_index("var")
    tile, at = lax.div(mine, per), lax.rem(mine, per)
    got = jnp.sum(got_ref[...], axis=0)
    lane = iota((pheno, LANE), 1)
    spots = [lax.rem(at * width + width + i, LANE) for i in range(3)]
    cross, square, cube = [row_sum(jnp.where(lane == spot, got, 0.0)) for spot in spots]
    norm0, noise = norm_ref[...][:, 0:1], cols_ref[1][:, 0:1]
    rate = cross / norm0
    alpha0 = 1.0 / (rate + noise)
    norm1 = alpha0 * alpha0 * (square - rate * cross)
    on_image, on_start = -alpha0, alpha0 * rate + norm1 / norm0
    both, first, last = on_image * on_image, 2.0 * on_image * on_start, on_start * on_start
    length = both * square + first * cross + last * norm0
    curve = both * cube + first * square + last * cross
    alpha1 = norm1 / (curve + noise * length)
    start = jnp.zeros((pheno, LANE), F32)
    image = jnp.zeros((pheno, LANE), F32)
    for t in range(rows // LANE):
        start = jnp.where(tile == t, cut(start_ref[...], t), start)
        image = jnp.where(tile == t, cut(image_ref[...], t), image)
    direction = on_image * image + on_start * start
    residual = -alpha0 * (image - rate * start) - alpha1 * (on_image * got + on_start * image + noise * direction)
    answer = alpha0 * start + alpha1 * direction
    out, left = answer[:, :width], residual[:, :width]
    for a in range(1, per):
        out = jnp.where(at == a, answer[:, a * width : (a + 1) * width], out)
        left = jnp.where(at == a, residual[:, a * width : (a + 1) * width], left)
    out_ref[...] = out
    residual_ref[...] = left


def exchange(x, axis, sets=None):
    return lax.all_to_all(x, axis, 0, 0, axis_index_groups=sets, tiled=True)


def shards(genotypes, imputed, centre, phenotypes, earlier, genetic, noise):
    rows, model = genotypes.shape
    other = imputed.shape[1]
    pheno = phenotypes.shape[0]
    groups, ways = lax.axis_size("samp"), lax.axis_size("var")
    span, side = model // groups, other // groups
    centre = centre[None, :]
    along = groups // (NEAR * CORES)
    at = lambda x, y, core: (x * NEAR + y) * CORES + core
    planes = [[at(x, y, core) for x in range(along) for core in range(CORES)] for y in range(NEAR)]
    lines = [[at(x, y, core) for y in range(NEAR)] for x in range(along) for core in range(CORES)]
    half = (16, model // 2)

    send, genotypes, cols = gather(groups, genotypes, imputed, centre, phenotypes, earlier, genetic, noise)
    got = exchange(send, "samp")
    owner = functools.partial(owner_kernel, float(rows * groups), span, side)
    tile = ((pheno, LANE), F32)
    send, keep, norm = call(owner, [((groups, 16, LANE), BF16), tile, tile], got, cols)
    got = exchange(send, "samp")
    back0 = functools.partial(back0_kernel, span, side)
    row, wide = ((1, model), F32), ((pheno, rows), F32)
    outs = [((ways, 16, rows // 2), BF16), wide, row, row]
    outs += [((pheno, model), F32), ((pheno, other), F32), tile]
    outs = call(back0, outs, got, genotypes, centre, phenotypes, keep, cols)
    send, start, mean, weight, back, scores, own = outs
    got = exchange(send, "var")
    outs = [((along * CORES,) + half, BF16), ((pheno, rows), F32)]
    send, image = call(project_kernel, outs, got, genotypes, mean)
    (send,) = call(middle_kernel, [((NEAR,) + half, BF16)], exchange(send, "samp", planes))
    got = exchange(send, "samp", lines)
    kept = (got, genotypes, mean, weight, back, own, cols, scores)
    out, sem = ((pheno, other), F32), (pltpu.SemaphoreType.DMA,)
    send, scores = call(back1_kernel, [((ways, pheno, LANE), F32)], *kept, out=out, scratch=sem)
    got = exchange(send, "var")
    part = ((pheno, rows // ways), F32)
    out, residual = call(finish_kernel, [part, part], got, start, image, norm, cols, make=jax.ShapeDtypeStruct)
    return (out, residual, scores)


def solution(mesh):
    in_specs = (
        P("samp", "var"),
        P("samp", "var"),
        P("samp"),
        P(None, "samp"),
        P(None, "samp"),
        P(),
        P(),
    )
    out_specs = (P(None, ("samp", "var")), P(None, ("samp", "var")), P(None, "var"))
    return jax.shard_map(shards, mesh=mesh, in_specs=in_specs, out_specs=out_specs, check_vma=False)
```

time: 102 us -> 100 us (0.980)
  blocking collectives: 93.5 us -> 91.8 us
    all_to_all x6, blocking collectives: 93.5 us -> 91.8 us  [exchange(): return lax.all_to_all(x, axis, 0, 0, axis_index_groups=sets, tiled=True)]
where the time goes in v5:
time: 100 us; the launch traced here: 98.8 us
  blocking collectives  91.8 us (92%)
  Pallas kernels  6.35 us (6%)
    all_to_all x6, blocking collectives, exchange(): return lax.all_to_all(x, axis, 0, 0, axis_index_groups=sets, tiled=True)  91.8 us
    pallas_call x6, Pallas kernels, call(): pl.pallas_call(kernel, out_shape=out_shape, in_specs=[pl.BlockSpec(memory...  3.6 us
    pallas_call x1, Pallas kernels, gather(): pl.pallas_call(gather_kernel, out_shape=[pltpu.VMEM((groups, 4, 5 * LANE)...  2.75 us

profile of v5, /device:TPU:1, one launch (start us, length us, event | category | flops | bytes accessed | tf_op | source)
XLA Modules:
  0.0 98.8 jit_solution(17222294970265750634)
XLA Ops:
  0.6 0.0 copy-start
  0.6 0.0 copy-start.1
  0.7 2.8 %shard_map.94 = (f32[32,4,640]{2,1,0:T(4,128)S(1)}, bf16[512,2560]{1,0:T(8,128)(2,1)S(1)}, f32[2,8,128]{2,1,0:T(8,128)S(1)}) custom-call(bf16[512,2560]{1,0:T(8,128)(2,1)} %gen_hbm.1, bf16[512,1280]{1,0:T(8,128)(2,1)} %imp_hbm.1, s32[1,512]{1,0:T(1,128)} %bitcast.1, f32[8,512]{1,0:T(8,128)} %phen_ref.1, f32[8,512]{1,0:T(8,128)} %earl_hbm.1, f32[8]{0:T(128)} %genetic_hbm.1, ...), custom_call_target="tpu_custom_call" | custom-call | tf_op jit(solution)/shard_map/pallas_call | solution.py:161
  3.4 22.3 %all_to_all.30.got_ref = f32[32,4,640]{2,1,0:T(4,128)S(1)} all-to-all(f32[32,4,640]{2,1,0:T(4,128)S(1)} %get-tuple-element.22), channel_id=1, replica_groups=mesh['samp'=32,'var'=16] {'samp'}, dimensions={0} | all-to-all | bytes 655360 | tf_op jit(solution)/shard_map/all_to_all | solution.py:411
  25.7 0.4 shard_map.95
  26.1 12.1 %all_to_all.31.got_ref = bf16[32,16,128]{2,1,0:T(8,128)(2,1)S(1)} all-to-all(bf16[32,16,128]{2,1,0:T(8,128)(2,1)S(1)} %get-tuple-element.24), channel_id=1, replica_groups=mesh['samp'=32,'var'=16] {'samp'}, dimensions={0} | all-to-all | bytes 262144 | tf_op jit(solution)/shard_map/all_to_all | solution.py:411
  38.2 0.0 copy-done
  38.2 0.0 copy-done.1
  38.2 0.8 shard_map.96
  39.0 23.7 %all_to_all.32.got_ref = bf16[16,16,256]{2,1,0:T(8,128)(2,1)S(1)} all-to-all(bf16[16,16,256]{2,1,0:T(8,128)(2,1)S(1)} %get-tuple-element.27), channel_id=1, replica_groups=mesh['samp'=32,'var'=16] {'var'}, dimensions={0} | all-to-all | bytes 262144 | tf_op jit(solution)/shard_map/all_to_all | solution.py:411
  62.7 0.5 shard_map.97
  63.2 11.6 %all_to_all.33.got_ref = bf16[8,16,1280]{2,1,0:T(8,128)(2,1)S(1)} all-to-all(bf16[8,16,1280]{2,1,0:T(8,128)(2,1)S(1)} %get-tuple-element.29), channel_id=1, replica_groups={{0,16,128,144,256,272,384,400},{32,48,160,176,288,304,416,432},{64,80,1..., dimensions={0} | all-to-all | bytes 655360 | tf_op jit(solution)/shard_map/all_to_all | solution.py:411
  74.8 8.0 %all_to_all.34.got_ref = bf16[4,16,1280]{2,1,0:T(8,128)(2,1)S(1)} all-to-all(bf16[4,16,1280]{2,1,0:T(8,128)(2,1)S(1)} %shard_map.98), channel_id=1, replica_groups={{0,32,64,96},{16,48,80,112},{128,160,192,224},{144,176,208,240},{256,28..., dimensions={0} | all-to-all | bytes 327680 | tf_op jit(solution)/shard_map/all_to_all | solution.py:411
  82.8 0.8 shard_map.99
  83.6 14.1 %all_to_all.35.got_ref = f32[16,8,128]{2,1,0:T(8,128)S(1)} all-to-all(f32[16,8,128]{2,1,0:T(8,128)S(1)} %get-tuple-element.34), channel_id=1, replica_groups=mesh['samp'=32,'var'=16] {'var'}, dimensions={0} | all-to-all | bytes 131072 | tf_op jit(solution)/shard_map/all_to_all | solution.py:411
  97.8 1.1 %shard_map.100 = (f32[8,32]{1,0:T(8,128)}, f32[8,32]{1,0:T(8,128)}) custom-call(f32[16,8,128]{2,1,0:T(8,128)S(1)} %all_to_all.35.got_ref, f32[8,512]{1,0:T(8,128)S(1)} %get-tuple-element.35.start_ref, f32[8,512]{1,0:T(8,128)S(1)} %get-tuple-element.36.image_ref, f32[8,128]{1,0:T(8,128)S(1)} %get-tuple-element.37.norm_ref, ...), custom_call_target="tpu_custom_call" | custom-call | tf_op jit(solution)/shard_map/pallas_call | solution.py:192
  (1 shorter events, 0.0 us)
Async XLA Ops:
  0.6 37.5 %copy-start = (f32[8,512]{1,0:T(8,128)S(1)}, f32[8,512]{1,0:T(8,128)}, u32[]{:S(2)}) copy-start(f32[8,512]{1,0:T(8,128)} %phen_ref.1) | copy-start | bytes 49156
  0.6 37.5 %copy-start.1 = (s32[512]{0:T(512)S(1)}, s32[512]{0:T(512)}, u32[]{:S(2)}) copy-start(s32[512]{0:T(512)} %param.9) | copy-start | bytes 6148

commit v6 on v5

--- a/solution.py
+++ b/solution.py
@@ -12,6 +12,7 @@
 SLOTS = 12
 LANE = 128
 BASE = 4096.0
+GRID = 64.0
 STEPS = 2
 GRANT = 16 << 20
 NEAR, CORES = 4, 2
@@ -204,10 +205,13 @@
     row, lane = iota((pheno, LANE), 0), iota((pheno, LANE), 1)
     pieces = [got_ref[:, :, at * LANE : (at + 1) * LANE] for at in range(5)]
     raw = [jnp.sum(x, axis=0) for x in pieces]
+    coarse = [jnp.floor(x * GRID) * (1.0 / GRID) for x in pieces[0:2]]
+    rest = jnp.concatenate([jnp.sum(x - y, axis=0) for x, y in zip(pieces[0:2], coarse)], axis=0)
+    coarse = jnp.concatenate([jnp.sum(y, axis=0) for y in coarse], axis=0)
     tops = [jnp.floor(x * (1.0 / BASE)) for x in pieces[2:]]
     low = jnp.concatenate([jnp.sum(x - BASE * y, axis=0) for x, y in zip(pieces[2:], tops)], axis=0)
     high = jnp.concatenate([jnp.sum(y, axis=0) for y in tops], axis=0)
-    product = jnp.concatenate(raw[0:2], axis=0)
+    product = coarse + rest
     table = jnp.concatenate(raw[2:4], axis=0)
     sums = jnp.where(lane < CENTRES, pltpu.roll(table, LANE - span, 1), 0.0)
     count = jnp.where(lane < CENTRES, pltpu.roll(table, LANE - span - CENTRES, 1), 0.0)
@@ -216,17 +220,19 @@
     extra = span + 2 * CENTRES
     within, first, second = [table[:, extra + at : extra + at + 1] for at in range(3)]
 
-    proj = product
+    mean_top = jnp.floor(centre_mean * GRID + 0.5) * (1.0 / GRID)
+    mean_rest = centre_mean - mean_top
     seen = jnp.zeros((1, LANE), F32)
     for c in range(CENTRES):
         line = low[c : c + 1] if c < SLOTS else high[c - SLOTS : c - SLOTS + 1]
         seen = seen + line
-        proj = proj - centre_mean[:, c : c + 1] * line
+        coarse = coarse - mean_top[:, c : c + 1] * line
+        rest = rest - mean_rest[:, c : c + 1] * line
     mean = seen / total
-    spread = high[CENTRES - SLOTS : CENTRES - SLOTS + 1] / total - mean * mean + 1e-05
-    scale = lax.rsqrt(spread)
-    proj = (proj - left * mean) * scale
-    back = proj * scale * cols_ref[0]
+    variance = high[CENTRES - SLOTS : CENTRES - SLOTS + 1] / total - mean * mean
+    spread = variance + 1e-05
+    scale = jnp.where(variance == 0.0, 0.0, lax.rsqrt(spread))
+    back = ((coarse + rest) - left * mean) * (scale * scale) * cols_ref[0]
     lines = jnp.zeros((pheno, LANE), F32)
     for at, line in enumerate(split(mean, 3) + split(scale * scale, 3) + split(spread, 2)):
         lines = jnp.where(row == at, line.astype(F32), lines)
@@ -239,8 +245,8 @@
 
     here, there = lane < span, lane < span + side
     top = jnp.where(here, back, jnp.where(there, score_top, 0.0))
-    rest = jnp.where(here, lines, jnp.where(there, score - score_top, 0.0))
-    send = jnp.concatenate([top, rest], axis=0).astype(BF16)
+    under = jnp.where(here, lines, jnp.where(there, score - score_top, 0.0))
+    send = jnp.concatenate([top, under], axis=0).astype(BF16)
     send_ref[...] = jnp.broadcast_to(send[None], (groups, 16, LANE))
     keep_ref[...] = centre_mean
 
@@ -314,8 +320,9 @@
     both = jnp.sum(got_ref[...].astype(F32), axis=0)
     image = jnp.concatenate([both[0:8], both[8:16]], axis=1)
     image_ref[...] = image
-    total = row_sum(image)
-    left = jnp.concatenate([p.astype(F32) for p in split(image, 2)], axis=0).astype(BF16)
+    pieces = [p.astype(F32) for p in split(image, 2)]
+    total = row_sum(pieces[0] + pieces[1])
+    left = jnp.concatenate(pieces, axis=0).astype(BF16)
     half = gen_ref.shape[1] // 2
     for at in range(0, half, 2 * LANE):
         parts = []
@@ -354,8 +361,9 @@
             back = proj * weight_ref[:, cols] * genetic
             new = new + proj * back
             mixed = mixed + proj * back_ref[:, cols]
-            shift = shift + back * mean_ref[:, cols]
-            low = jnp.concatenate([p.astype(F32) for p in split(back, 2)], axis=0).astype(BF16)
+            pieces = [p.astype(F32) for p in split(back, 2)]
+            shift = shift + (pieces[0] + pieces[1]) * mean_ref[:, cols]
+            low = jnp.concatenate(pieces, axis=0).astype(BF16)
             part = dot_t(low, gen_ref[:, cols])
             acc = part if acc is None else acc + part
     part = acc[0:8] + acc[8:16] - row_sum(shift)

time: 100 us -> 100 us (level)
  no operation moved by 1% of the time
where the time goes in v6:
time: 100 us; the launch traced here: 98.9 us
  blocking collectives  91.8 us (92%)
  Pallas kernels  6.44 us (6%)
    all_to_all x6, blocking collectives, exchange(): return lax.all_to_all(x, axis, 0, 0, axis_index_groups=sets, tiled=True)  91.8 us
    pallas_call x6, Pallas kernels, call(): pl.pallas_call(kernel, out_shape=out_shape, in_specs=[pl.BlockSpec(memory...  3.69 us
    pallas_call x1, Pallas kernels, gather(): pl.pallas_call(gather_kernel, out_shape=[pltpu.VMEM((groups, 4, 5 * LANE)...  2.75 us

profile of v6, /device:TPU:1, one launch (start us, length us, event | category | flops | bytes accessed | tf_op | source)
XLA Modules:
  0.0 98.9 jit_solution(13116527968772566847)
XLA Ops:
  0.6 0.0 copy-start
  0.6 0.0 copy-start.1
  0.7 2.8 %shard_map.94 = (f32[32,4,640]{2,1,0:T(4,128)S(1)}, bf16[512,2560]{1,0:T(8,128)(2,1)S(1)}, f32[2,8,128]{2,1,0:T(8,128)S(1)}) custom-call(bf16[512,2560]{1,0:T(8,128)(2,1)} %gen_hbm.1, bf16[512,1280]{1,0:T(8,128)(2,1)} %imp_hbm.1, s32[1,512]{1,0:T(1,128)} %bitcast.1, f32[8,512]{1,0:T(8,128)} %phen_ref.1, f32[8,512]{1,0:T(8,128)} %earl_hbm.1, f32[8]{0:T(128)} %genetic_hbm.1, ...), custom_call_target="tpu_custom_call" | custom-call | tf_op jit(solution)/shard_map/pallas_call | solution.py:162
  3.4 22.3 %all_to_all.30.got_ref = f32[32,4,640]{2,1,0:T(4,128)S(1)} all-to-all(f32[32,4,640]{2,1,0:T(4,128)S(1)} %get-tuple-element.22), channel_id=1, replica_groups=mesh['samp'=32,'var'=16] {'samp'}, dimensions={0} | all-to-all | bytes 655360 | tf_op jit(solution)/shard_map/all_to_all | solution.py:419
  25.7 0.5 shard_map.95
  26.2 12.1 %all_to_all.31.got_ref = bf16[32,16,128]{2,1,0:T(8,128)(2,1)S(1)} all-to-all(bf16[32,16,128]{2,1,0:T(8,128)(2,1)S(1)} %get-tuple-element.24), channel_id=1, replica_groups=mesh['samp'=32,'var'=16] {'samp'}, dimensions={0} | all-to-all | bytes 262144 | tf_op jit(solution)/shard_map/all_to_all | solution.py:419
  38.2 0.0 copy-done
  38.2 0.0 copy-done.1
  38.2 0.8 shard_map.96
  39.1 23.7 %all_to_all.32.got_ref = bf16[16,16,256]{2,1,0:T(8,128)(2,1)S(1)} all-to-all(bf16[16,16,256]{2,1,0:T(8,128)(2,1)S(1)} %get-tuple-element.27), channel_id=1, replica_groups=mesh['samp'=32,'var'=16] {'var'}, dimensions={0} | all-to-all | bytes 262144 | tf_op jit(solution)/shard_map/all_to_all | solution.py:419
  62.8 0.5 shard_map.97
  63.3 11.6 %all_to_all.33.got_ref = bf16[8,16,1280]{2,1,0:T(8,128)(2,1)S(1)} all-to-all(bf16[8,16,1280]{2,1,0:T(8,128)(2,1)S(1)} %get-tuple-element.29), channel_id=1, replica_groups={{0,16,128,144,256,272,384,400},{32,48,160,176,288,304,416,432},{64,80,1..., dimensions={0} | all-to-all | bytes 655360 | tf_op jit(solution)/shard_map/all_to_all | solution.py:419
  74.9 8.0 %all_to_all.34.got_ref = bf16[4,16,1280]{2,1,0:T(8,128)(2,1)S(1)} all-to-all(bf16[4,16,1280]{2,1,0:T(8,128)(2,1)S(1)} %shard_map.98), channel_id=1, replica_groups={{0,32,64,96},{16,48,80,112},{128,160,192,224},{144,176,208,240},{256,28..., dimensions={0} | all-to-all | bytes 327680 | tf_op jit(solution)/shard_map/all_to_all | solution.py:419
  82.9 0.8 shard_map.99
  83.7 14.1 %all_to_all.35.got_ref = f32[16,8,128]{2,1,0:T(8,128)S(1)} all-to-all(f32[16,8,128]{2,1,0:T(8,128)S(1)} %get-tuple-element.34), channel_id=1, replica_groups=mesh['samp'=32,'var'=16] {'var'}, dimensions={0} | all-to-all | bytes 131072 | tf_op jit(solution)/shard_map/all_to_all | solution.py:419
  97.8 1.1 %shard_map.100 = (f32[8,32]{1,0:T(8,128)}, f32[8,32]{1,0:T(8,128)}) custom-call(f32[16,8,128]{2,1,0:T(8,128)S(1)} %all_to_all.35.got_ref, f32[8,512]{1,0:T(8,128)S(1)} %get-tuple-element.35.start_ref, f32[8,512]{1,0:T(8,128)S(1)} %get-tuple-element.36.image_ref, f32[8,128]{1,0:T(8,128)S(1)} %get-tuple-element.37.norm_ref, ...), custom_call_target="tpu_custom_call" | custom-call | tf_op jit(solution)/shard_map/pallas_call | solution.py:193
  (1 shorter events, 0.0 us)
Async XLA Ops:
  0.6 37.6 %copy-start = (f32[8,512]{1,0:T(8,128)S(1)}, f32[8,512]{1,0:T(8,128)}, u32[]{:S(2)}) copy-start(f32[8,512]{1,0:T(8,128)} %phen_ref.1) | copy-start | bytes 49156
  0.6 37.6 %copy-start.1 = (s32[512]{0:T(512)S(1)}, s32[512]{0:T(512)}, u32[]{:S(2)}) copy-start(s32[512]{0:T(512)} %param.9) | copy-start | bytes 6148

commit v7 on v6

--- a/solution.py
+++ b/solution.py
@@ -407,12 +407,9 @@
     direction = on_image * image + on_start * start
     residual = -alpha0 * (image - rate * start) - alpha1 * (on_image * got + on_start * image + noise * direction)
     answer = alpha0 * start + alpha1 * direction
-    out, left = answer[:, :width], residual[:, :width]
-    for a in range(1, per):
-        out = jnp.where(at == a, answer[:, a * width : (a + 1) * width], out)
-        left = jnp.where(at == a, residual[:, a * width : (a + 1) * width], left)
-    out_ref[...] = out
-    residual_ref[...] = left
+    turn = lax.rem(LANE - at * width, LANE)
+    out_ref[...] = pltpu.roll(answer, turn, 1)[:, :width]
+    residual_ref[...] = pltpu.roll(residual, turn, 1)[:, :width]
 
 
 def exchange(x, axis, sets=None):

time: 100 us -> 99.9 us (level)
  no operation moved by 1% of the time
where the time goes in v7:
time: 99.9 us; the launch traced here: 98.7 us
  blocking collectives  91.8 us (92%)
  Pallas kernels  6.24 us (6%)
    all_to_all x6, blocking collectives, exchange(): return lax.all_to_all(x, axis, 0, 0, axis_index_groups=sets, tiled=True)  91.8 us
    pallas_call x6, Pallas kernels, call(): pl.pallas_call(kernel, out_shape=out_shape, in_specs=[pl.BlockSpec(memory...  3.48 us
    pallas_call x1, Pallas kernels, gather(): pl.pallas_call(gather_kernel, out_shape=[pltpu.VMEM((groups, 4, 5 * LANE)...  2.75 us

profile of v7, /device:TPU:1, one launch (start us, length us, event | category | flops | bytes accessed | tf_op | source)
XLA Modules:
  0.0 98.7 jit_solution(8641784160866461951)
XLA Ops:
  0.6 0.0 copy-start
  0.6 0.0 copy-start.1
  0.7 2.8 %shard_map.94 = (f32[32,4,640]{2,1,0:T(4,128)S(1)}, bf16[512,2560]{1,0:T(8,128)(2,1)S(1)}, f32[2,8,128]{2,1,0:T(8,128)S(1)}) custom-call(bf16[512,2560]{1,0:T(8,128)(2,1)} %gen_hbm.1, bf16[512,1280]{1,0:T(8,128)(2,1)} %imp_hbm.1, s32[1,512]{1,0:T(1,128)} %bitcast.1, f32[8,512]{1,0:T(8,128)} %phen_ref.1, f32[8,512]{1,0:T(8,128)} %earl_hbm.1, f32[8]{0:T(128)} %genetic_hbm.1, ...), custom_call_target="tpu_custom_call" | custom-call | tf_op jit(solution)/shard_map/pallas_call | solution.py:162
  3.4 22.3 %all_to_all.30.got_ref = f32[32,4,640]{2,1,0:T(4,128)S(1)} all-to-all(f32[32,4,640]{2,1,0:T(4,128)S(1)} %get-tuple-element.22), channel_id=1, replica_groups=mesh['samp'=32,'var'=16] {'samp'}, dimensions={0} | all-to-all | bytes 655360 | tf_op jit(solution)/shard_map/all_to_all | solution.py:416
  25.7 0.5 shard_map.95
  26.2 12.1 %all_to_all.31.got_ref = bf16[32,16,128]{2,1,0:T(8,128)(2,1)S(1)} all-to-all(bf16[32,16,128]{2,1,0:T(8,128)(2,1)S(1)} %get-tuple-element.24), channel_id=1, replica_groups=mesh['samp'=32,'var'=16] {'samp'}, dimensions={0} | all-to-all | bytes 262144 | tf_op jit(solution)/shard_map/all_to_all | solution.py:416
  38.2 0.0 copy-done
  38.2 0.0 copy-done.1
  38.2 0.8 shard_map.96
  39.1 23.7 %all_to_all.32.got_ref = bf16[16,16,256]{2,1,0:T(8,128)(2,1)S(1)} all-to-all(bf16[16,16,256]{2,1,0:T(8,128)(2,1)S(1)} %get-tuple-element.27), channel_id=1, replica_groups=mesh['samp'=32,'var'=16] {'var'}, dimensions={0} | all-to-all | bytes 262144 | tf_op jit(solution)/shard_map/all_to_all | solution.py:416
  62.8 0.5 shard_map.97
  63.3 11.6 %all_to_all.33.got_ref = bf16[8,16,1280]{2,1,0:T(8,128)(2,1)S(1)} all-to-all(bf16[8,16,1280]{2,1,0:T(8,128)(2,1)S(1)} %get-tuple-element.29), channel_id=1, replica_groups={{0,16,128,144,256,272,384,400},{32,48,160,176,288,304,416,432},{64,80,1..., dimensions={0} | all-to-all | bytes 655360 | tf_op jit(solution)/shard_map/all_to_all | solution.py:416
  74.9 8.0 %all_to_all.34.got_ref = bf16[4,16,1280]{2,1,0:T(8,128)(2,1)S(1)} all-to-all(bf16[4,16,1280]{2,1,0:T(8,128)(2,1)S(1)} %shard_map.98), channel_id=1, replica_groups={{0,32,64,96},{16,48,80,112},{128,160,192,224},{144,176,208,240},{256,28..., dimensions={0} | all-to-all | bytes 327680 | tf_op jit(solution)/shard_map/all_to_all | solution.py:416
  82.9 0.8 shard_map.99
  83.7 14.1 %all_to_all.35.got_ref = f32[16,8,128]{2,1,0:T(8,128)S(1)} all-to-all(f32[16,8,128]{2,1,0:T(8,128)S(1)} %get-tuple-element.34), channel_id=1, replica_groups=mesh['samp'=32,'var'=16] {'var'}, dimensions={0} | all-to-all | bytes 131072 | tf_op jit(solution)/shard_map/all_to_all | solution.py:416
  97.8 0.9 shard_map.100
  (1 shorter events, 0.0 us)
Async XLA Ops:
  0.6 37.6 %copy-start = (f32[8,512]{1,0:T(8,128)S(1)}, f32[8,512]{1,0:T(8,128)}, u32[]{:S(2)}) copy-start(f32[8,512]{1,0:T(8,128)} %phen_ref.1) | copy-start | bytes 49156
  0.6 37.6 %copy-start.1 = (s32[512]{0:T(512)S(1)}, s32[512]{0:T(512)}, u32[]{:S(2)}) copy-start(s32[512]{0:T(512)} %param.9) | copy-start | bytes 6148
